TPU v7x, 32 devices: a whole 2x2x4 slice. The times are simulated.
32 devices in a mesh: gx: 8 (over z, x), gy: 4 (over y, core).
Axes of the slice: x: 2, y: 2, z: 4, core: 2. Of those that a mesh axis runs over, the one named last changes fastest.
Arguments:
- tiles: float32 [23, 8, 4, 2, 128, 128], P(None, 'gx', 'gy'), may hold values from -0.006 to 0.006
- chi: float32 [8, 4, 2, 128], P('gx', 'gy'), may hold values from -12 to 12
- species: int32 [8, 4, 2, 128], P('gx', 'gy'), may hold values from 0 to 3
- counts: int32 [8, 4, 2], P('gx', 'gy'), may hold values from 64 to 128, as said below
- hardness: float32 [4], replicated, may hold values from 1.25 to 2.5
Outputs:
- charges: float32 [8, 4, 2, 128], P('gx', 'gy')
- residual: float32 [8, 4, 2, 128], P('gx', 'gy')
Inputs may be any that keep to these rules, and one draw needn't show every extreme that they name: `counts`: every draw has a block with exactly 128 atoms and one with exactly 64.
All inputs are finite; a program needn't handle non-finite values.
Results may differ from a plain program's by a relative error of at most 0.0003.
Values sent between devices are 32-bit elements; how exact they have to be, the bound alone decides.
No kernel may reach another device: no remote copies, remote signals or barrier semaphores. Data moves between devices by JAX's collectives and lax.ppermute only.
A program may use at most 64 MiB of HBM per device.

v0:
```python
import jax
import jax.numpy as jnp
from jax import lax
from jax.sharding import PartitionSpec as P

ITERS = 3


exact_mode = lax.Precision.HIGHEST


def extended_2(block, sides, width):
    for axis, dim in sides:
        count = lax.axis_size(axis)
        forward = [(i, i + 1) for i in range(count - 1)]
        forward.append((count - 1, 0))
        backward = [(target, source) for source, target in forward]
        low = lax.ppermute(
            lax.slice_in_dim(block, block.shape[dim] - width, None, axis=dim), axis, forward
        )
        high = lax.ppermute(lax.slice_in_dim(block, 0, width, axis=dim), axis, backward)
        block = jnp.concatenate([low, block, high], axis=dim)
    return block


def shifted(value, axis, steps):
    count = lax.axis_size(axis)
    pairs = [(source, (source + steps) % count) for source in range(count)]
    return lax.ppermute(value, axis, pairs)


def forward_offsets():
    offsets = [(0, 0, 0), (0, 0, 1), (0, 1, -1), (0, 1, 0), (0, 1, 1)]
    for shift_x in (1, 2):
        for shift_y in (-1, 0, 1):
            for shift_z in (-1, 0, 1):
                offsets.append((shift_x, shift_y, shift_z))
    return offsets


def wrap_cells(cell_block):
    return jnp.concatenate([cell_block[..., -1:, :], cell_block, cell_block[..., :1, :]], axis=-2)


def row_halo(values):
    return extended_2(values[None], (("gy", 0),), 1)


def inner_sums(partial_value):
    return lax.psum(partial_value, ("gx", "gy"))


def apply_half(values, own_tiles, diagonal, occupied, offsets):
    cell_count = values.shape[0]
    row_block = row_halo(values)
    slab_list = [row_block] + [shifted(row_block, "gx", -reach_x) for reach_x in (1, 2)]
    extended = wrap_cells(jnp.stack(slab_list))
    fronts = jnp.stack(
        [
            extended[shift_x, 1 + shift_y, 1 + shift_z : 1 + shift_z + cell_count]
            for shift_x, shift_y, shift_z in offsets
        ]
    )
    summed = jnp.einsum("kzab,kzb->za", own_tiles, fronts, precision=exact_mode)
    returned = jnp.einsum("kzab,za->kzb", own_tiles, values, precision=exact_mode)
    summed = summed + returned[0]
    grouped = [[jnp.zeros_like(values) for lift_y in range(3)] for reach_x in range(3)]
    for offset_index in range(1, len(offsets)):
        shift_x, shift_y, shift_z = offsets[offset_index]
        grouped[shift_x][shift_y + 1] = grouped[shift_x][shift_y + 1] + jnp.roll(
            returned[offset_index], shift_z, axis=0
        )
    lifted = grouped[0]
    for reach_x in (1, 2):
        arrived = shifted(jnp.stack(grouped[reach_x]), "gx", reach_x)
        lifted = [lifted[lift_y] + arrived[lift_y] for lift_y in range(3)]
    summed = summed + lifted[1]
    for lift_y in (1, -1):
        summed = summed + shifted(lifted[lift_y + 1], "gy", lift_y)
    return occupied * (diagonal * values + summed)


def body(tiles, chi, species, counts, hardness):
    offsets = forward_offsets()
    own_tiles = tiles[:, 0, 0]
    cell_count = chi.shape[2]
    slot_count = chi.shape[3]
    occupied = (
        lax.broadcasted_iota(jnp.int32, (cell_count, slot_count), 1) < counts[0, 0][:, None]
    ).astype(jnp.float32)
    diagonal = jnp.zeros((cell_count, slot_count), jnp.float32)
    for element in range(hardness.shape[0]):
        diagonal = diagonal + jnp.where(species[0, 0] == element, hardness[element], 0.0)
    residual = -chi[0, 0] * occupied
    charges = jnp.zeros_like(residual)
    direction = residual
    norm_now = inner_sums(jnp.sum(residual * residual))
    for iteration in range(ITERS):
        applied = apply_half(direction, own_tiles, diagonal, occupied, offsets)
        step_size = norm_now / inner_sums(jnp.sum(direction * applied))
        charges = charges + step_size * direction
        residual = residual - step_size * applied
        if iteration + 1 < ITERS:
            norm_next = inner_sums(jnp.sum(residual * residual))
            direction = residual + norm_next / norm_now * direction
            norm_now = norm_next
    return (charges[None, None], residual[None, None])


def solution(mesh):
    in_specs = (
        P(None, "gx", "gy", None, None, None),
        P("gx", "gy", None, None),
        P("gx", "gy", None, None),
        P("gx", "gy", None),
        P(),
    )
    out_specs = (P("gx", "gy", None, None), P("gx", "gy", None, None))
    return jax.shard_map(body, mesh=mesh, in_specs=in_specs, out_specs=out_specs, check_vma=False)
```

profile of v0, /device:TPU:0, one launch (start us, length us, event | category | flops | bytes accessed | tf_op | source)
XLA Modules:
  0.0 266.3 jit_solution(10091793245459492928)
XLA Ops:
  0.6 0.0 copy-start
  0.7 0.9 compare_select_fusion
  1.6 0.5 collective-permute-start
  2.1 1.9 collective-permute-start.1
  4.0 0.8 bitcast_select_fusion
  4.8 0.0 copy-start.4
  4.8 1.6 fusion.8
  6.4 2.3 collective-permute-start.4
  8.8 1.6 collective-permute-start.5
  10.4 0.7 fusion.89
  11.0 0.0 collective-permute-done.1
  11.0 3.3 %collective-permute-start.2 = (f32[3,2,128]{2,1,0:T(2,128)S(1)}, f32[3,2,128]{2,1,0:T(2,128)S(1)}, u32[]{:S(2)}, u32[]{:S(2)}) collective-permute-start(f32[3,2,128]{2,1,0:T(2,128)S(1)} %pad_maximum_fusion.3), channel_id=1, source_target_pairs={{0,28},{4,0},{8,4},{12,8},{16,12},{20,16},{24,20},{28,24},{1,29},{... | collective-permute-start | bytes 9224 | tf_op jit(solution)/shard_map/ppermute | solution.py:29
  14.3 0.3 collective-permute-start.3
  14.7 0.0 collective-permute-done.5
  14.7 0.1 collective-permute-start.6
  14.8 1.7 collective-permute-start.7
  16.5 0.0 collective-permute-done.2
  16.5 1.4 collective-permute-done.3
  18.3 2.7 %fusion.10 = f32[2,1,128,1]{2,1,3,0:T(1,128)S(1)} fusion(f32[23,2,128,1]{2,1,0,3:T(2,128)S(1)} %bitcast.720, f32[23,1,1,2,128,128]{5,4,3,2,1,0:T(8,128)S(1)} %copy-done), kind=kOutput, calls=%fused_computation.10 | convolution fusion | flops 9043968 | bytes 3039232 | tf_op jit(solution)/shard_map/kzab,kzb->za/dot_general | solution.py:64
  21.0 0.0 collective-permute-done.6
  21.0 0.0 copy-done.1
  21.0 3.4 %multiply_reduce_fusion.4 = (f32[]{:T(128)}, f32[]{:T(128)}, f32[2,128]{1,0:T(2,128)S(1)}, f32[2,128]{1,0:T(2,128)S(1)}) fusion(f32[2,128]{1,0:T(2,128)S(1)} %collective-permute-done.7, f32[2,128]{1,0:T(2,128)S(1)} %collective-permute-done.6, f32[3,2,128]{2,1,0:T(2,128)S(1)} %collective-permute-done.5, f32[3,2,128]{2,1,0:T(2,128)S(1)} %collective-permute-done.4, ...), kind=kLoop, calls=%fused_computation.299 | loop fusion | flops 7166 | bytes 11296 | tf_op jit(solution)/shard_map/reduce_sum | solution.py:100
  24.4 38.3 %all-reduce = (f32[]{:T(128)}, f32[]{:T(128)}) all-reduce(f32[]{:T(128)} %get-tuple-element.3, f32[]{:T(128)} %get-tuple-element.2), channel_id=1, replica_groups=mesh['gx'=8,'gy'=4] {'gx','gy'}, use_global_device_ids=true, to_apply=%region_1.2 | all-reduce | flops 2 | bytes 16 | tf_op jit(solution)/shard_map/psum | solution.py:50
  64.0 0.7 multiply_reduce_fusion.3
  64.6 41.5 %psum.44 = f32[]{:T(128)} all-reduce(f32[]{:T(128)} %multiply_reduce_fusion.3), channel_id=1, replica_groups=mesh['gx'=8,'gy'=4] {'gx','gy'}, use_global_device_ids=true, to_apply=%region_5.6 | all-reduce | flops 1 | bytes 8 | tf_op jit(solution)/shard_map/psum | solution.py:50
  107.5 0.1 multiply_add_fusion.1
  107.6 1.7 collective-permute-start.9
  109.3 1.6 fusion.4
  111.0 2.3 collective-permute-start.12
  113.3 0.2 collective-permute-start.13
  113.5 0.0 collective-permute-done.8
  113.5 0.0 collective-permute-done.9
  113.6 3.2 %collective-permute-start.10 = (f32[3,2,128]{2,1,0:T(2,128)S(1)}, f32[3,2,128]{2,1,0:T(2,128)S(1)}, u32[]{:S(2)}, u32[]{:S(2)}) collective-permute-start(f32[3,2,128]{2,1,0:T(2,128)S(1)} %pad_maximum_fusion.6), channel_id=1, source_target_pairs={{0,28},{4,0},{8,4},{12,8},{16,12},{20,16},{24,20},{28,24},{1,29},{... | collective-permute-start | bytes 9224 | tf_op jit(solution)/shard_map/ppermute | solution.py:29
  116.7 1.1 collective-permute-start.11
  117.9 0.0 collective-permute-done.12
  117.9 0.8 collective-permute-done.13
  118.7 0.1 collective-permute-start.14
  118.8 1.7 collective-permute-start.15
  120.6 0.0 collective-permute-done.10
  120.6 0.0 collective-permute-done.11
  120.9 2.7 %fusion.6 = f32[2,1,128,1]{2,1,3,0:T(1,128)S(1)} fusion(f32[23,2,128,1]{2,1,0,3:T(2,128)S(1)} %bitcast.721, f32[23,1,1,2,128,128]{5,4,3,2,1,0:T(8,128)S(1)} %copy-done), kind=kOutput, calls=%fused_computation.6 | convolution fusion | flops 9043968 | bytes 3039232 | tf_op jit(solution)/shard_map/kzab,kzb->za/dot_general | solution.py:64
  123.6 0.0 collective-permute-done.14
  123.6 0.0 collective-permute-done.15
  123.6 0.7 multiply_reduce_fusion.2
  124.3 38.8 %psum.45 = f32[]{:T(128)} all-reduce(f32[]{:T(128)} %get-tuple-element.10), channel_id=1, replica_groups=mesh['gx'=8,'gy'=4] {'gx','gy'}, use_global_device_ids=true, to_apply=%region_7.8 | all-reduce | flops 1 | bytes 8 | tf_op jit(solution)/shard_map/psum | solution.py:50
  164.5 0.7 multiply_reduce_fusion.1
  165.1 42.4 %psum.46 = f32[]{:T(128)} all-reduce(f32[]{:T(128)} %get-tuple-element.8), channel_id=1, replica_groups=mesh['gx'=8,'gy'=4] {'gx','gy'}, use_global_device_ids=true, to_apply=%region_9.10 | all-reduce | flops 1 | bytes 8 | tf_op jit(solution)/shard_map/psum | solution.py:50
  208.9 0.1 collective-permute-start.16
  209.0 1.7 collective-permute-start.17
  210.7 1.6 fusion
  212.4 2.3 collective-permute-start.20
  214.7 0.0 collective-permute-start.21
  214.7 0.0 collective-permute-done.16
  214.8 3.4 %collective-permute-start.18 = (f32[3,2,128]{2,1,0:T(2,128)S(1)}, f32[3,2,128]{2,1,0:T(2,128)S(1)}, u32[]{:S(2)}, u32[]{:S(2)}) collective-permute-start(f32[3,2,128]{2,1,0:T(2,128)S(1)} %pad_maximum_fusion.9), channel_id=1, source_target_pairs={{0,28},{4,0},{8,4},{12,8},{16,12},{20,16},{24,20},{28,24},{1,29},{... | collective-permute-start | bytes 9224 | tf_op jit(solution)/shard_map/ppermute | solution.py:29
  218.1 1.1 collective-permute-start.19
  219.3 0.0 collective-permute-done.20
  219.3 0.8 collective-permute-done.21
  220.1 0.1 collective-permute-start.22
  220.2 1.7 collective-permute-start.23
  221.9 0.0 collective-permute-done.18
  222.3 2.7 %fusion.2 = f32[2,1,128,1]{2,1,3,0:T(1,128)S(1)} fusion(f32[23,2,128,1]{2,1,0,3:T(2,128)S(1)} %bitcast.722, f32[23,1,1,2,128,128]{5,4,3,2,1,0:T(8,128)S(1)} %copy-done), kind=kOutput, calls=%fused_computation.2 | convolution fusion | flops 9043968 | bytes 3039232 | tf_op jit(solution)/shard_map/kzab,kzb->za/dot_general | solution.py:64
  225.0 0.7 multiply_reduce_fusion
  225.7 38.7 %psum.47 = f32[]{:T(128)} all-reduce(f32[]{:T(128)} %get-tuple-element.6), channel_id=1, replica_groups=mesh['gx'=8,'gy'=4] {'gx','gy'}, use_global_device_ids=true, to_apply=%region_11.12 | all-reduce | flops 1 | bytes 8 | tf_op jit(solution)/shard_map/psum | solution.py:50
  265.7 0.6 subtract_bitcast_fusion
  (124 shorter events, 1.3 us)
Async XLA Ops:
  0.6 4.1 %copy-start = (f32[23,1,1,2,128,128]{5,4,3,2,1,0:T(8,128)S(1)}, f32[23,1,1,2,128,128]{5,4,3,2,1,0:T(8,128)}, u32[]{:S(2)}) copy-start(f32[23,1,1,2,128,128]{5,4,3,2,1,0:T(8,128)} %param.5) | copy-start | bytes 9043972
  0.6 9.7 %copy-start.3 = (f32[4]{0:T(128)S(1)}, f32[4]{0:T(128)}, u32[]{:S(2)}) copy-start(f32[4]{0:T(128)} %param.9) | copy-start | bytes 52
  1.6 9.5 %collective-permute-start = (f32[1,2,128]{2,1,0:T(2,128)S(1)}, f32[1,2,128]{2,1,0:T(2,128)S(1)}, u32[]{:S(2)}, u32[]{:S(2)}) collective-permute-start(f32[1,2,128]{2,1,0:T(2,128)S(1)} %compare_select_fusion), channel_id=1, source_target_pairs={{0,1},{1,2},{2,3},{3,0},{4,5},{5,6},{6,7},{7,4},{8,9},{9,10},{10,1... | collective-permute-start | bytes 3080 | tf_op jit(solution)/shard_map/ppermute | solution.py:18
  2.1 9.0 %collective-permute-start.1 = (f32[1,2,128]{2,1,0:T(2,128)S(1)}, f32[1,2,128]{2,1,0:T(2,128)S(1)}, u32[]{:S(2)}, u32[]{:S(2)}) collective-permute-start(f32[1,2,128]{2,1,0:T(2,128)S(1)} %compare_select_fusion), channel_id=1, source_target_pairs={{1,0},{2,1},{3,2},{0,3},{5,4},{6,5},{7,6},{4,7},{9,8},{10,9},{11,1... | collective-permute-start | bytes 3080 | tf_op jit(solution)/shard_map/ppermute | solution.py:21
  4.8 16.2 %copy-start.1 = (f32[1,1,2,128]{3,2,1,0:T(2,128)S(1)}, f32[1,1,2,128]{3,2,1,0:T(2,128)}, u32[]{:S(2)}) copy-start(f32[1,1,2,128]{3,2,1,0:T(2,128)} %param.6) | copy-start | bytes 3076
  4.8 16.2 %copy-start.2 = (s32[1,1,2]{2,1,0:T(1,128)S(1)}, s32[1,1,2]{2,1,0:T(1,128)}, u32[]{:S(2)}) copy-start(s32[1,1,2]{2,1,0:T(1,128)} %param.8) | copy-start | bytes 28
  4.8 16.2 %copy-start.4 = (s32[1,1,2,128]{3,2,1,0:T(2,128)S(1)}, s32[1,1,2,128]{3,2,1,0:T(2,128)}, u32[]{:S(2)}) copy-start(s32[1,1,2,128]{3,2,1,0:T(2,128)} %param.7) | copy-start | bytes 3076
  6.4 8.2 %collective-permute-start.4 = (f32[3,2,128]{2,1,0:T(2,128)S(1)}, f32[3,2,128]{2,1,0:T(2,128)S(1)}, u32[]{:S(2)}, u32[]{:S(2)}) collective-permute-start(f32[3,2,128]{2,1,0:T(2,128)S(1)} %pad_maximum_fusion.4), channel_id=1, source_target_pairs={{0,4},{4,8},{8,12},{12,16},{16,20},{20,24},{24,28},{28,0},{1,5},{5... | collective-permute-start | bytes 9224 | tf_op jit(solution)/shard_map/ppermute | solution.py:29
  8.8 5.9 %collective-permute-start.5 = (f32[3,2,128]{2,1,0:T(2,128)S(1)}, f32[3,2,128]{2,1,0:T(2,128)S(1)}, u32[]{:S(2)}, u32[]{:S(2)}) collective-permute-start(f32[3,2,128]{2,1,0:T(2,128)S(1)} %pad_maximum_fusion.5), channel_id=1, source_target_pairs={{0,8},{4,12},{8,16},{12,20},{16,24},{20,28},{24,0},{28,4},{1,9},{5... | collective-permute-start | bytes 9224 | tf_op jit(solution)/shard_map/ppermute | solution.py:29
  11.0 5.5 %collective-permute-start.2 = (f32[3,2,128]{2,1,0:T(2,128)S(1)}, f32[3,2,128]{2,1,0:T(2,128)S(1)}, u32[]{:S(2)}, u32[]{:S(2)}) collective-permute-start(f32[3,2,128]{2,1,0:T(2,128)S(1)} %pad_maximum_fusion.3), channel_id=1, source_target_pairs={{0,28},{4,0},{8,4},{12,8},{16,12},{20,16},{24,20},{28,24},{1,29},{... | collective-permute-start | bytes 9224 | tf_op jit(solution)/shard_map/ppermute | solution.py:29
  14.3 3.6 %collective-permute-start.3 = (f32[3,2,128]{2,1,0:T(2,128)S(1)}, f32[3,2,128]{2,1,0:T(2,128)S(1)}, u32[]{:S(2)}, u32[]{:S(2)}) collective-permute-start(f32[3,2,128]{2,1,0:T(2,128)S(1)} %pad_maximum_fusion.3), channel_id=1, source_target_pairs={{0,24},{4,28},{8,0},{12,4},{16,8},{20,12},{24,16},{28,20},{1,25},{... | collective-permute-start | bytes 9224 | tf_op jit(solution)/shard_map/ppermute | solution.py:29
  14.7 6.2 %collective-permute-start.6 = (f32[2,128]{1,0:T(2,128)S(1)}, f32[2,128]{1,0:T(2,128)S(1)}, u32[]{:S(2)}, u32[]{:S(2)}) collective-permute-start(f32[2,128]{1,0:T(2,128)S(1)} %fusion.60), channel_id=1, source_target_pairs={{0,1},{1,2},{2,3},{3,0},{4,5},{5,6},{6,7},{7,4},{8,9},{9,10},{10,1... | collective-permute-start | bytes 3080 | tf_op jit(solution)/shard_map/ppermute | solution.py:29
  14.8 6.2 %collective-permute-start.7 = (f32[2,128]{1,0:T(2,128)S(1)}, f32[2,128]{1,0:T(2,128)S(1)}, u32[]{:S(2)}, u32[]{:S(2)}) collective-permute-start(f32[2,128]{1,0:T(2,128)S(1)} %fusion.59), channel_id=1, source_target_pairs={{0,3},{1,0},{2,1},{3,2},{4,7},{5,4},{6,5},{7,6},{8,11},{9,8},{10,9... | collective-permute-start | bytes 3080 | tf_op jit(solution)/shard_map/ppermute | solution.py:29
  107.6 6.0 %collective-permute-start.8 = (f32[1,2,128]{2,1,0:T(2,128)S(1)}, f32[1,2,128]{2,1,0:T(2,128)S(1)}, u32[]{:S(2)}, u32[]{:S(2)}) collective-permute-start(f32[1,2,128]{2,1,0:T(2,128)S(1)} %bitcast.701), channel_id=1, source_target_pairs={{0,1},{1,2},{2,3},{3,0},{4,5},{5,6},{6,7},{7,4},{8,9},{9,10},{10,1... | collective-permute-start | bytes 3080 | tf_op jit(solution)/shard_map/ppermute | solution.py:18
  107.6 6.0 %collective-permute-start.9 = (f32[1,2,128]{2,1,0:T(2,128)S(1)}, f32[1,2,128]{2,1,0:T(2,128)S(1)}, u32[]{:S(2)}, u32[]{:S(2)}) collective-permute-start(f32[1,2,128]{2,1,0:T(2,128)S(1)} %bitcast.702), channel_id=1, source_target_pairs={{1,0},{2,1},{3,2},{0,3},{5,4},{6,5},{7,6},{4,7},{9,8},{10,9},{11,1... | collective-permute-start | bytes 3080 | tf_op jit(solution)/shard_map/ppermute | solution.py:21
  111.0 6.9 %collective-permute-start.12 = (f32[3,2,128]{2,1,0:T(2,128)S(1)}, f32[3,2,128]{2,1,0:T(2,128)S(1)}, u32[]{:S(2)}, u32[]{:S(2)}) collective-permute-start(f32[3,2,128]{2,1,0:T(2,128)S(1)} %pad_maximum_fusion.7), channel_id=1, source_target_pairs={{0,4},{4,8},{8,12},{12,16},{16,20},{20,24},{24,28},{28,0},{1,5},{5... | collective-permute-start | bytes 9224 | tf_op jit(solution)/shard_map/ppermute | solution.py:29
  113.3 5.4 %collective-permute-start.13 = (f32[3,2,128]{2,1,0:T(2,128)S(1)}, f32[3,2,128]{2,1,0:T(2,128)S(1)}, u32[]{:S(2)}, u32[]{:S(2)}) collective-permute-start(f32[3,2,128]{2,1,0:T(2,128)S(1)} %pad_maximum_fusion.8), channel_id=1, source_target_pairs={{0,8},{4,12},{8,16},{12,20},{16,24},{20,28},{24,0},{28,4},{1,9},{5... | collective-permute-start | bytes 9224 | tf_op jit(solution)/shard_map/ppermute | solution.py:29
  113.6 7.0 %collective-permute-start.10 = (f32[3,2,128]{2,1,0:T(2,128)S(1)}, f32[3,2,128]{2,1,0:T(2,128)S(1)}, u32[]{:S(2)}, u32[]{:S(2)}) collective-permute-start(f32[3,2,128]{2,1,0:T(2,128)S(1)} %pad_maximum_fusion.6), channel_id=1, source_target_pairs={{0,28},{4,0},{8,4},{12,8},{16,12},{20,16},{24,20},{28,24},{1,29},{... | collective-permute-start | bytes 9224 | tf_op jit(solution)/shard_map/ppermute | solution.py:29
  116.7 3.8 %collective-permute-start.11 = (f32[3,2,128]{2,1,0:T(2,128)S(1)}, f32[3,2,128]{2,1,0:T(2,128)S(1)}, u32[]{:S(2)}, u32[]{:S(2)}) collective-permute-start(f32[3,2,128]{2,1,0:T(2,128)S(1)} %pad_maximum_fusion.6), channel_id=1, source_target_pairs={{0,24},{4,28},{8,0},{12,4},{16,8},{20,12},{24,16},{28,20},{1,25},{... | collective-permute-start | bytes 9224 | tf_op jit(solution)/shard_map/ppermute | solution.py:29
  118.7 4.8 %collective-permute-start.14 = (f32[2,128]{1,0:T(2,128)S(1)}, f32[2,128]{1,0:T(2,128)S(1)}, u32[]{:S(2)}, u32[]{:S(2)}) collective-permute-start(f32[2,128]{1,0:T(2,128)S(1)} %fusion.40), channel_id=1, source_target_pairs={{0,1},{1,2},{2,3},{3,0},{4,5},{5,6},{6,7},{7,4},{8,9},{9,10},{10,1... | collective-permute-start | bytes 3080 | tf_op jit(solution)/shard_map/ppermute | solution.py:29
  118.8 4.8 %collective-permute-start.15 = (f32[2,128]{1,0:T(2,128)S(1)}, f32[2,128]{1,0:T(2,128)S(1)}, u32[]{:S(2)}, u32[]{:S(2)}) collective-permute-start(f32[2,128]{1,0:T(2,128)S(1)} %fusion.39), channel_id=1, source_target_pairs={{0,3},{1,0},{2,1},{3,2},{4,7},{5,4},{6,5},{7,6},{8,11},{9,8},{10,9... | collective-permute-start | bytes 3080 | tf_op jit(solution)/shard_map/ppermute | solution.py:29
  208.9 5.8 %collective-permute-start.16 = (f32[1,2,128]{2,1,0:T(2,128)S(1)}, f32[1,2,128]{2,1,0:T(2,128)S(1)}, u32[]{:S(2)}, u32[]{:S(2)}) collective-permute-start(f32[1,2,128]{2,1,0:T(2,128)S(1)} %bitcast.715), channel_id=1, source_target_pairs={{0,1},{1,2},{2,3},{3,0},{4,5},{5,6},{6,7},{7,4},{8,9},{9,10},{10,1... | collective-permute-start | bytes 3080 | tf_op jit(solution)/shard_map/ppermute | solution.py:18
  209.0 5.8 %collective-permute-start.17 = (f32[1,2,128]{2,1,0:T(2,128)S(1)}, f32[1,2,128]{2,1,0:T(2,128)S(1)}, u32[]{:S(2)}, u32[]{:S(2)}) collective-permute-start(f32[1,2,128]{2,1,0:T(2,128)S(1)} %bitcast.716), channel_id=1, source_target_pairs={{1,0},{2,1},{3,2},{0,3},{5,4},{6,5},{7,6},{4,7},{9,8},{10,9},{11,1... | collective-permute-start | bytes 3080 | tf_op jit(solution)/shard_map/ppermute | solution.py:21
  212.4 6.9 %collective-permute-start.20 = (f32[3,2,128]{2,1,0:T(2,128)S(1)}, f32[3,2,128]{2,1,0:T(2,128)S(1)}, u32[]{:S(2)}, u32[]{:S(2)}) collective-permute-start(f32[3,2,128]{2,1,0:T(2,128)S(1)} %pad_maximum_fusion.10), channel_id=1, source_target_pairs={{0,4},{4,8},{8,12},{12,16},{16,20},{20,24},{24,28},{28,0},{1,5},{5... | collective-permute-start | bytes 9224 | tf_op jit(solution)/shard_map/ppermute | solution.py:29
  214.7 5.4 %collective-permute-start.21 = (f32[3,2,128]{2,1,0:T(2,128)S(1)}, f32[3,2,128]{2,1,0:T(2,128)S(1)}, u32[]{:S(2)}, u32[]{:S(2)}) collective-permute-start(f32[3,2,128]{2,1,0:T(2,128)S(1)} %pad_maximum_fusion.11), channel_id=1, source_target_pairs={{0,8},{4,12},{8,16},{12,20},{16,24},{20,28},{24,0},{28,4},{1,9},{5... | collective-permute-start | bytes 9224 | tf_op jit(solution)/shard_map/ppermute | solution.py:29
  214.8 7.2 %collective-permute-start.18 = (f32[3,2,128]{2,1,0:T(2,128)S(1)}, f32[3,2,128]{2,1,0:T(2,128)S(1)}, u32[]{:S(2)}, u32[]{:S(2)}) collective-permute-start(f32[3,2,128]{2,1,0:T(2,128)S(1)} %pad_maximum_fusion.9), channel_id=1, source_target_pairs={{0,28},{4,0},{8,4},{12,8},{16,12},{20,16},{24,20},{28,24},{1,29},{... | collective-permute-start | bytes 9224 | tf_op jit(solution)/shard_map/ppermute | solution.py:29
  218.1 3.8 %collective-permute-start.19 = (f32[3,2,128]{2,1,0:T(2,128)S(1)}, f32[3,2,128]{2,1,0:T(2,128)S(1)}, u32[]{:S(2)}, u32[]{:S(2)}) collective-permute-start(f32[3,2,128]{2,1,0:T(2,128)S(1)} %pad_maximum_fusion.9), channel_id=1, source_target_pairs={{0,24},{4,28},{8,0},{12,4},{16,8},{20,12},{24,16},{28,20},{1,25},{... | collective-permute-start | bytes 9224 | tf_op jit(solution)/shard_map/ppermute | solution.py:29
  220.1 4.8 %collective-permute-start.22 = (f32[2,128]{1,0:T(2,128)S(1)}, f32[2,128]{1,0:T(2,128)S(1)}, u32[]{:S(2)}, u32[]{:S(2)}) collective-permute-start(f32[2,128]{1,0:T(2,128)S(1)} %fusion.20), channel_id=1, source_target_pairs={{0,1},{1,2},{2,3},{3,0},{4,5},{5,6},{6,7},{7,4},{8,9},{9,10},{10,1... | collective-permute-start | bytes 3080 | tf_op jit(solution)/shard_map/ppermute | solution.py:29
  220.2 4.8 %collective-permute-start.23 = (f32[2,128]{1,0:T(2,128)S(1)}, f32[2,128]{1,0:T(2,128)S(1)}, u32[]{:S(2)}, u32[]{:S(2)}) collective-permute-start(f32[2,128]{1,0:T(2,128)S(1)} %fusion.19), channel_id=1, source_target_pairs={{0,3},{1,0},{2,1},{3,2},{4,7},{5,4},{6,5},{7,6},{8,11},{9,8},{10,9... | collective-permute-start | bytes 3080 | tf_op jit(solution)/shard_map/ppermute | solution.py:29
where the time goes:
time: 268 us; the launch traced here: 266 us
  blocking collectives  200 us (75%)
  starting transfers between devices  32.5 us (12%)
  matrix products  12.7 us (5%)
  other arithmetic  9.34 us (3%)
  between operations  7.87 us (3%)
  waiting for transfers between devices  3.16 us (1%)
    psum x5, blocking collectives, inner_sums(): return lax.psum(partial_value, ('gx', 'gy'))  200 us
    ppermute x18, starting transfers between devices, shifted(): return lax.ppermute(value, axis, pairs)  26.5 us
    dot_general x3, matrix products, apply_half(): summed = jnp.einsum('kzab,kzb->za', own_tiles, fronts, precision=exact_mode)  8 us
    ppermute x3, starting transfers between devices, extended_2(): lax.ppermute(lax.slice_in_dim(block, 0, width, axis=dim), axis, backward)  5.42 us
  transfers between devices with their start and end apart: 24, of which 3 were waited for; matrix products, arithmetic and copies ran while one was open for 6% of the time, Pallas kernels for 0%

commit v1 on v0

v1 whole, which is shorter than its diff:
```python
import functools

import jax
import jax.numpy as jnp
from jax import lax
from jax.experimental import pallas as pl
from jax.experimental.pallas import tpu as pltpu
from jax.sharding import PartitionSpec as P

AHEAD = ((0, 1), (1, -1), (1, 0), (1, 1), (2, -1), (2, 0), (2, 1))


def forward_offsets():
    offsets = [(0, 0, 0), (0, 0, 1), (0, 1, -1), (0, 1, 0), (0, 1, 1)]
    for shift_x in (1, 2):
        for shift_y in (-1, 0, 1):
            for shift_z in (-1, 0, 1):
                offsets.append((shift_x, shift_y, shift_z))
    return offsets


def neighbours(grid):
    count_x, count_y = grid
    here_x, here_y = lax.axis_index("gx"), lax.axis_index("gy")
    ahead, behind = [], []
    for shift_x, shift_y in AHEAD:
        for sign, found in ((1, ahead), (-1, behind)):
            along_x = lax.rem(here_x + (sign * shift_x) % count_x, count_x)
            along_y = lax.rem(here_y + (sign * shift_y) % count_y, count_y)
            found.append(along_x * count_y + along_y)
    return ahead, behind


def rows_of(value):
    return [value[cell : cell + 1] for cell in range(value.shape[0])]


def transposed_products(tiles_ref, value):
    cells, slots = value.shape
    sums = {}
    for cell in range(cells):
        column = jnp.broadcast_to(value[cell : cell + 1], (slots, slots)).T
        for index, (shift_x, shift_y, shift_z) in enumerate(forward_offsets()):
            product = tiles_ref[index, cell] * column
            part = product.reshape(slots // 8, 8, slots).sum(0)
            key = (shift_x, shift_y), (cell + shift_z) % cells
            sums[key] = sums[key] + part if key in sums else part
    sums = {key: jnp.sum(part, axis=0, keepdims=True) for key, part in sums.items()}
    return {
        row: jnp.concatenate([sums[row, cell] for cell in range(cells)], axis=0)
        for row in ((0, 0),) + AHEAD
    }


def direct_products(tiles_ref, rows):
    cells, slots = rows[0, 0].shape
    split = {row: rows_of(value) for row, value in rows.items()}
    found = []
    for cell in range(cells):
        total = None
        for index, (shift_x, shift_y, shift_z) in enumerate(forward_offsets()):
            reached = split[shift_x, shift_y][(cell + shift_z) % cells]
            product = tiles_ref[index, cell] * reached
            total = product if total is None else total + product
        found.append(jnp.sum(total.T, axis=0, keepdims=True))
    return jnp.concatenate(found, axis=0)


def occupied_of(counts_ref, shape):
    slot = lax.broadcasted_iota(jnp.int32, shape, 1)
    cell = lax.broadcasted_iota(jnp.int32, shape, 0)
    filled = jnp.zeros(shape, jnp.int32)
    for place in range(shape[0]):
        filled = jnp.where(cell == place, counts_ref[place], filled)
    return slot < filled


def pack(grid, send_ref, tiles_ref, value, own_ref):
    cells = value.shape[0]
    ahead, behind = neighbours(grid)
    sent = transposed_products(tiles_ref, value)
    for place, row in enumerate(AHEAD):
        send_ref[ahead[place], :cells, :] = sent[row]
        send_ref[behind[place], :cells, :] = value
    own_ref[...] = sent[0, 0]


def pack_sums(send_ref, residual, image):
    cells = residual.shape[0]
    first = jnp.sum(residual * residual, axis=0, keepdims=True)
    second = jnp.sum(residual * image, axis=0, keepdims=True)
    both = jnp.concatenate([first, second], axis=0)
    count = send_ref.shape[0]
    send_ref[:, cells : cells + 2, :] = jnp.broadcast_to(both[None], (count,) + both.shape)


def total_sums(received_ref, cells):
    lanes = jnp.sum(received_ref[:, cells : cells + 2, :], axis=0)
    sums = jnp.sum(lanes, axis=1, keepdims=True)
    return sums[0:1], sums[1:2]


def applied(grid, tiles_ref, received_ref, value, own, diagonal, occupied):
    cells = value.shape[0]
    ahead, behind = neighbours(grid)
    rows = {(0, 0): value}
    total = diagonal * value + own
    for place, row in enumerate(AHEAD):
        rows[row] = received_ref[ahead[place], :cells, :]
        total = total + received_ref[behind[place], :cells, :]
    total = total + direct_products(tiles_ref, rows)
    return jnp.where(occupied, total, 0.0)


def start_kernel(grid, tiles_ref, chi_ref, counts_ref, send_ref, own_ref, residual_ref):
    chi = chi_ref[...]
    residual = jnp.where(occupied_of(counts_ref, chi.shape), -chi, 0.0)
    residual_ref[...] = residual
    send_ref[...] = jnp.zeros_like(send_ref)
    pack(grid, send_ref, tiles_ref, residual, own_ref)


def first_kernel(
    grid, tiles_ref, received_ref, residual_ref, own_ref, species_ref, hardness_ref, counts_ref,
    send_ref, next_own_ref, image_ref, diagonal_ref,
):
    residual = residual_ref[...]
    species = species_ref[...]
    diagonal = jnp.zeros_like(residual)
    for element in range(hardness_ref.shape[0]):
        diagonal = diagonal + jnp.where(species == element, hardness_ref[element], 0.0)
    diagonal_ref[...] = diagonal
    occupied = occupied_of(counts_ref, residual.shape)
    image = applied(grid, tiles_ref, received_ref, residual, own_ref[...], diagonal, occupied)
    image_ref[...] = image
    send_ref[...] = jnp.zeros_like(send_ref)
    pack_sums(send_ref, residual, image)
    pack(grid, send_ref, tiles_ref, image, next_own_ref)


def second_kernel(
    grid, tiles_ref, received_ref, residual_ref, image_ref, own_ref, diagonal_ref, counts_ref,
    send_ref, next_own_ref, second_ref, next_residual_ref, next_image_ref, sums_ref,
):
    residual, image = residual_ref[...], image_ref[...]
    occupied = occupied_of(counts_ref, residual.shape)
    second = applied(
        grid, tiles_ref, received_ref, image, own_ref[...], diagonal_ref[...], occupied
    )
    norm, curvature = total_sums(received_ref, residual.shape[0])
    step = norm / curvature
    next_residual = residual - step * image
    next_image = image - step * second
    second_ref[...] = second
    next_residual_ref[...] = next_residual
    next_image_ref[...] = next_image
    sums_ref[0:1] = jnp.broadcast_to(norm, (1, sums_ref.shape[1]))
    sums_ref[1:2] = jnp.broadcast_to(curvature, (1, sums_ref.shape[1]))
    send_ref[...] = jnp.zeros_like(send_ref)
    pack_sums(send_ref, next_residual, next_image)
    pack(grid, send_ref, tiles_ref, next_image, next_own_ref)


def third_kernel(
    grid, tiles_ref, received_ref, first_residual_ref, first_image_ref, residual_ref, image_ref,
    second_ref, own_ref, diagonal_ref, counts_ref, sums_ref,
    send_ref, charges_ref, direction_ref, push_ref, next_residual_ref, next_image_ref, next_sums_ref,
):
    residual, image = residual_ref[...], image_ref[...]
    cells, slots = residual.shape
    occupied = occupied_of(counts_ref, residual.shape)
    second = applied(
        grid, tiles_ref, received_ref, image, own_ref[...], diagonal_ref[...], occupied
    )
    old_norm, old_curvature = sums_ref[0:1, 0:1], sums_ref[1:2, 0:1]
    norm, product = total_sums(received_ref, cells)
    ratio = norm / old_norm
    curvature = product - ratio * ratio * old_curvature
    step = norm / curvature
    direction = residual + ratio * first_residual_ref[...]
    push = image + ratio * first_image_ref[...]
    bend = second + ratio * second_ref[...]
    charges_ref[...] = (old_norm / old_curvature) * first_residual_ref[...] + step * direction
    next_residual = residual - step * push
    next_image = image - step * bend
    direction_ref[...] = direction
    push_ref[...] = push
    next_residual_ref[...] = next_residual
    next_image_ref[...] = next_image
    next_sums_ref[0:1] = jnp.broadcast_to(norm, (1, slots))
    next_sums_ref[1:2] = jnp.broadcast_to(curvature, (1, slots))
    first = jnp.sum(next_residual * next_residual, axis=0, keepdims=True)
    last = jnp.sum(next_residual * next_image, axis=0, keepdims=True)
    both = jnp.concatenate([first, last], axis=0)
    send_ref[...] = jnp.broadcast_to(both[None], send_ref.shape)


def last_kernel(
    received_ref, charges_ref, direction_ref, push_ref, residual_ref, image_ref, sums_ref,
    out_charges_ref, out_residual_ref,
):
    residual = residual_ref[...]
    old_norm, old_curvature = sums_ref[0:1, 0:1], sums_ref[1:2, 0:1]
    norm, product = total_sums(received_ref, 0)
    ratio = norm / old_norm
    curvature = product - ratio * ratio * old_curvature
    step = norm / curvature
    direction = residual + ratio * direction_ref[...]
    push = image_ref[...] + ratio * push_ref[...]
    out_charges_ref[...] = charges_ref[...] + step * direction
    out_residual_ref[...] = residual - step * push


def body(tiles, chi, species, counts, hardness):
    grid = lax.axis_size("gx"), lax.axis_size("gy")
    count = grid[0] * grid[1]
    own_tiles = tiles[:, 0, 0]
    cells, slots = chi.shape[2:]
    vmem = pl.BlockSpec(memory_space=pltpu.VMEM)
    smem = pl.BlockSpec(memory_space=pltpu.SMEM)
    value = jax.ShapeDtypeStruct((cells, slots), jnp.float32)
    pair = jax.ShapeDtypeStruct((2, slots), jnp.float32)
    message = jax.ShapeDtypeStruct((count, cells + 2, slots), jnp.float32)
    short = jax.ShapeDtypeStruct((count, 2, slots), jnp.float32)

    def call(kernel, outputs, specs):
        return pl.pallas_call(
            kernel,
            out_shape=outputs,
            in_specs=specs,
            out_specs=[vmem] * len(outputs),
            compiler_params=pltpu.CompilerParams(vmem_limit_bytes=24 * 2**20),
        )

    def exchange(buffer):
        return lax.all_to_all(buffer, ("gx", "gy"), 0, 0, tiled=True)

    own_counts = counts[0, 0]
    send, own, residual0 = call(
        functools.partial(start_kernel, grid), (message, value, value), [vmem, vmem, smem]
    )(own_tiles, chi[0, 0], own_counts)
    received = exchange(send)
    send, own, image0, diagonal = call(
        functools.partial(first_kernel, grid),
        (message, value, value, value),
        [vmem] * 5 + [smem] * 2,
    )(own_tiles, received, residual0, own, species[0, 0], hardness, own_counts)
    received = exchange(send)
    send, own, second, residual, image, sums = call(
        functools.partial(second_kernel, grid),
        (message, value, value, value, value, pair),
        [vmem] * 6 + [smem],
    )(own_tiles, received, residual0, image0, own, diagonal, own_counts)
    received = exchange(send)
    send, charges, direction, push, residual, image, sums = call(
        functools.partial(third_kernel, grid),
        (short, value, value, value, value, value, pair),
        [vmem] * 9 + [smem, vmem],
    )(
        own_tiles, received, residual0, image0, residual, image, second, own, diagonal,
        own_counts, sums,
    )
    received = exchange(send)
    charges, residual = call(last_kernel, (value, value), [vmem] * 7)(
        received, charges, direction, push, residual, image, sums
    )
    return charges[None, None], residual[None, None]


def solution(mesh):
    in_specs = (
        P(None, "gx", "gy", None, None, None),
        P("gx", "gy", None, None),
        P("gx", "gy", None, None),
        P("gx", "gy", None),
        P(),
    )
    out_specs = (P("gx", "gy", None, None), P("gx", "gy", None, None))
    return jax.shard_map(body, mesh=mesh, in_specs=in_specs, out_specs=out_specs, check_vma=False)
```

time: 268 us -> 50.8 us (0.19)
  blocking collectives: 200 us -> 41.7 us
  starting transfers between devices: 32.5 us -> 0 us
  matrix products: 12.7 us -> 0 us
  other arithmetic: 9.34 us -> 0 us
  between operations: 7.87 us -> 0.7 us
  Pallas kernels: 0 us -> 4.98 us
  waiting for transfers between devices: 3.16 us -> 0 us
    psum x5 -> x0, blocking collectives: 200 us -> none  [inner_sums(): return lax.psum(partial_value, ('gx', 'gy'))]
    all_to_all x0 -> x4, blocking collectives: none -> 41.7 us  [exchange(): return lax.all_to_all(buffer, ('gx', 'gy'), 0, 0, tiled=True)]
    ppermute x24 -> x0, starting transfers between devices: 32.5 us -> none  [the longest x18 26.5 us: shifted(): return lax.ppermute(value, axis, pairs)]
    dot_general x6 -> x0, matrix products: 12.7 us -> none  [the longest x3 8 us: apply_half(): summed = jnp.einsum('kzab,kzb->za', own_tiles, fronts, precision=exact_mode)]
    reduce_sum x5 -> x0, other arithmetic: 6.05 us -> none  [the longest x3 4.71 us: body(): step_size = norm_now / inner_sums(jnp.sum(direction * applied))]
    pallas_call x0 -> x5, Pallas kernels: none -> 4.98 us  [the longest x1 1.23 us: body(): call(functools.partial(second_kernel, grid), (message, value, value, valu...]
    ppermute x24 -> x0, waiting for transfers between devices: 3.16 us -> none  [the longest x18 3.15 us: shifted(): return lax.ppermute(value, axis, pairs)]
    unnamed x34 -> x12, local copies, waits for them, and re-layouts: 0.23 us -> 3.21 us
  transfers between devices with their start and end apart: 24 -> 0, of which waited for: 3 -> 0; matrix products, arithmetic and copies ran while one was open for 6% -> 0% of each run, Pallas kernels for 0% -> 0%
where the time goes in v1:
time: 50.8 us; the launch traced here: 50.6 us
  blocking collectives  41.7 us (82%)
  Pallas kernels  4.98 us (10%)
  local copies, waits for them, and re-layouts  3.21 us (6%)
  between operations  0.7 us (1%)
    all_to_all x4, blocking collectives, exchange(): return lax.all_to_all(buffer, ('gx', 'gy'), 0, 0, tiled=True)  41.7 us
    unnamed x12, local copies, waits for them, and re-layouts  3.21 us
    pallas_call x1, Pallas kernels, body(): call(functools.partial(second_kernel, grid), (message, value, value, valu...  1.23 us
    pallas_call x1, Pallas kernels, body(): call(functools.partial(first_kernel, grid), (message, value, value, value...  1.23 us

profile of v1, /device:TPU:0, one launch (start us, length us, event | category | flops | bytes accessed | tf_op | source)
XLA Modules:
  0.0 50.6 jit_solution(1440650590704291413)
XLA Ops:
  0.6 0.0 copy-start.2
  0.6 0.0 copy-start.5
  0.7 0.0 copy-start.4
  0.7 0.0 copy-start
  0.7 1.9 %copy-done = f32[23,1,1,2,128,128]{5,4,3,2,1,0:T(8,128)S(1)} copy-done((f32[23,1,1,2,128,128]{5,4,3,2,1,0:T(8,128)S(1)}, f32[23,1,1,2,128,128]{5,4,3,2,1,0:T(8,128)}, u32[]{:S(2)}) %copy-start) | copy-done | bytes 3014680
  2.5 0.0 copy-start.1
  2.5 0.7 %copy-done.1 = s32[1,1,2]{2,1,0:T(1,128)S(1)} copy-done((s32[1,1,2]{2,1,0:T(1,128)S(1)}, s32[1,1,2]{2,1,0:T(1,128)}, u32[]{:S(2)}) %copy-start.1) | copy-done | bytes 32
  3.2 0.0 copy-start.3
  3.2 0.7 %copy-done.3 = f32[1,1,2,128]{3,2,1,0:T(2,128)S(1)} copy-done((f32[1,1,2,128]{3,2,1,0:T(2,128)S(1)}, f32[1,1,2,128]{3,2,1,0:T(2,128)}, u32[]{:S(2)}) %copy-start.3) | copy-done | bytes 1048
  3.9 0.9 %shard_map.68 = (f32[32,4,128]{2,1,0:T(4,128)S(1)}, f32[2,128]{1,0:T(2,128)S(1)}, f32[2,128]{1,0:T(2,128)S(1)}) custom-call(f32[23,2,128,128]{3,2,1,0:T(8,128)S(1)} %bitcast.6, f32[2,128]{1,0:T(2,128)S(1)} %bitcast.14, s32[2]{0:T(128)S(1)} %bitcast.10), custom_call_target="tpu_custom_call" | custom-call | tf_op jit(solution)/shard_map/pallas_call | solution.py:239
  4.8 14.5 %all_to_all.20.received_ref = f32[32,4,128]{2,1,0:T(4,128)S(1)} all-to-all(f32[32,4,128]{2,1,0:T(4,128)S(1)} %get-tuple-element.24), channel_id=1, replica_groups=mesh['gx'=8,'gy'=4] {'gx','gy'}, dimensions={0} | all-to-all | bytes 131072 | tf_op jit(solution)/shard_map/all_to_all | solution.py:236
  19.3 0.0 copy-done.2
  19.3 0.0 copy-done.5
  19.3 0.0 copy-done.4
  19.3 1.2 %shard_map.69 = (f32[32,4,128]{2,1,0:T(4,128)S(1)}, f32[2,128]{1,0:T(2,128)S(1)}, f32[2,128]{1,0:T(2,128)S(1)}, f32[2,128]{1,0:T(2,128)S(1)}) custom-call(f32[23,2,128,128]{3,2,1,0:T(8,128)S(1)} %bitcast.7, f32[32,4,128]{2,1,0:T(4,128)S(1)} %all_to_all.20.received_ref, f32[2,128]{1,0:T(2,128)S(1)} %get-tuple-element.25.residual_ref.first_residual_ref, ...), custom_call_target="tpu_custom_call" | custom-call | tf_op jit(solution)/shard_map/pallas_call | solution.py:243
  20.6 9.1 %all_to_all.21.received_ref = f32[32,4,128]{2,1,0:T(4,128)S(1)} all-to-all(f32[32,4,128]{2,1,0:T(4,128)S(1)} %get-tuple-element.27), channel_id=1, replica_groups=mesh['gx'=8,'gy'=4] {'gx','gy'}, dimensions={0} | all-to-all | bytes 131072 | tf_op jit(solution)/shard_map/all_to_all | solution.py:236
  29.7 1.2 %shard_map.70 = (f32[32,4,128]{2,1,0:T(4,128)S(1)}, f32[2,128]{1,0:T(2,128)S(1)}, f32[2,128]{1,0:T(2,128)S(1)}, f32[2,128]{1,0:T(2,128)S(1)}, f32[2,128]{1,0:T(2,128)S(1)}, /*index=5*/f32[2,128]{1,0:T(2,128)S(1)}) custom-call(f32[23,2,128,128]{3,2,1,0:T(8,128)S(1)} %bitcast.8, f32[32,4,128]{2,1,0:T(4,128)S(1)} %all_to_all.21.received_ref, ...), custom_call_target="tpu_custom_call" | custom-call | tf_op jit(solution)/shard_map/pallas_call | solution.py:249
  30.9 9.1 %all_to_all.22.received_ref = f32[32,4,128]{2,1,0:T(4,128)S(1)} all-to-all(f32[32,4,128]{2,1,0:T(4,128)S(1)} %get-tuple-element.31), channel_id=1, replica_groups=mesh['gx'=8,'gy'=4] {'gx','gy'}, dimensions={0} | all-to-all | bytes 131072 | tf_op jit(solution)/shard_map/all_to_all | solution.py:236
  40.0 0.9 %shard_map.71 = (f32[32,2,128]{2,1,0:T(2,128)S(1)}, f32[2,128]{1,0:T(2,128)S(1)}, f32[2,128]{1,0:T(2,128)S(1)}, f32[2,128]{1,0:T(2,128)S(1)}, f32[2,128]{1,0:T(2...) custom-call(f32[23,2,128,128]{3,2,1,0:T(8,128)S(1)} %bitcast.9, f32[32,4,128]{2,1,0:T(4,128)S(1)} %all_to_all.22.received_ref, ...), custom_call_target="tpu_custom_call" | custom-call | tf_op jit(solution)/shard_map/pallas_call | solution.py:255
  40.9 9.0 %all_to_all.23.received_ref = f32[32,2,128]{2,1,0:T(2,128)S(1)} all-to-all(f32[32,2,128]{2,1,0:T(2,128)S(1)} %get-tuple-element.37), channel_id=1, replica_groups=mesh['gx'=8,'gy'=4] {'gx','gy'}, dimensions={0} | all-to-all | bytes 65536 | tf_op jit(solution)/shard_map/all_to_all | solution.py:236
  49.9 0.7 %shard_map.72 = (f32[2,128]{1,0:T(2,128)}, f32[2,128]{1,0:T(2,128)}) custom-call(f32[32,2,128]{2,1,0:T(2,128)S(1)} %all_to_all.23.received_ref, f32[2,128]{1,0:T(2,128)S(1)} %get-tuple-element.38.charges_ref, f32[2,128]{1,0:T(2,128)S(1)} %get-tuple-element.39.direction_ref, f32[2,128]{1,0:T(2,128)S(1)} %get-tuple-element.40.push_ref, ...), custom_call_target="tpu_custom_call" | custom-call | tf_op jit(solution)/shard_map/pallas_call | solution.py:264
Async XLA Ops:
  0.6 18.7 %copy-start.2 = (s32[1,1,2]{2,1,0:T(1,128)S(1)}, s32[1,1,2]{2,1,0:T(1,128)}, u32[]{:S(2)}) copy-start(s32[1,1,2]{2,1,0:T(1,128)} %param.8) | copy-start | bytes 28
  0.6 18.7 %copy-start.5 = (f32[4]{0:T(128)S(1)}, f32[4]{0:T(128)}, u32[]{:S(2)}) copy-start(f32[4]{0:T(128)} %hardness_ref.1) | copy-start | bytes 52
  0.7 18.7 %copy-start.4 = (s32[1,1,2,128]{3,2,1,0:T(2,128)S(1)}, s32[1,1,2,128]{3,2,1,0:T(2,128)}, u32[]{:S(2)}) copy-start(s32[1,1,2,128]{3,2,1,0:T(2,128)} %param.7) | copy-start | bytes 3076
  0.7 1.9 %copy-start = (f32[23,1,1,2,128,128]{5,4,3,2,1,0:T(8,128)S(1)}, f32[23,1,1,2,128,128]{5,4,3,2,1,0:T(8,128)}, u32[]{:S(2)}) copy-start(f32[23,1,1,2,128,128]{5,4,3,2,1,0:T(8,128)} %param.5) | copy-start | bytes 9043972
  2.5 0.7 %copy-start.1 = (s32[1,1,2]{2,1,0:T(1,128)S(1)}, s32[1,1,2]{2,1,0:T(1,128)}, u32[]{:S(2)}) copy-start(s32[1,1,2]{2,1,0:T(1,128)} %param.8) | copy-start | bytes 28
  3.2 0.7 %copy-start.3 = (f32[1,1,2,128]{3,2,1,0:T(2,128)S(1)}, f32[1,1,2,128]{3,2,1,0:T(2,128)}, u32[]{:S(2)}) copy-start(f32[1,1,2,128]{3,2,1,0:T(2,128)} %param.6) | copy-start | bytes 3076

commit v2 on v0

v2 whole, which is shorter than its diff:
```python
import functools

import jax
import jax.numpy as jnp
from jax import lax
from jax.experimental import pallas as pl
from jax.experimental.pallas import tpu as pltpu
from jax.sharding import PartitionSpec as P

AHEAD = ((0, 1), (1, -1), (1, 0), (1, 1), (2, -1), (2, 0), (2, 1))
ROWS = ((0, 0),) + AHEAD
SUMS = ("vv", "vr", "vw", "rr", "rw", "ww", "vAv", "vAr", "vAw", "rAr", "rAw", "wAw")
FOLD = 8


def forward_offsets():
    offsets = [(0, 0, 0), (0, 0, 1), (0, 1, -1), (0, 1, 0), (0, 1, 1)]
    for shift_x in (1, 2):
        for shift_y in (-1, 0, 1):
            for shift_z in (-1, 0, 1):
                offsets.append((shift_x, shift_y, shift_z))
    return offsets


def reached_cells(cells):
    places = {}
    for index, (shift_x, shift_y, shift_z) in enumerate(forward_offsets()):
        places.setdefault(((shift_x, shift_y), shift_z % cells), []).append(index)
    return list(places.items())


def neighbours(grid):
    count_x, count_y = grid
    here_x, here_y = lax.axis_index("gx"), lax.axis_index("gy")
    ahead, behind = [], []
    for shift_x, shift_y in AHEAD:
        for sign, found in ((1, ahead), (-1, behind)):
            along_x = lax.rem(here_x + (sign * shift_x) % count_x, count_x)
            along_y = lax.rem(here_y + (sign * shift_y) % count_y, count_y)
            found.append(along_x * count_y + along_y)
    return ahead, behind


def columns_of(value):
    slots = value.shape[1]
    return [
        jnp.broadcast_to(value[cell : cell + 1], (slots, slots)).T
        for cell in range(value.shape[0])
    ]


def add_transposed(sums, place, cell, cells, tile, column):
    slots = tile.shape[0]
    part = (tile * column).reshape(slots // 8, 8, slots).sum(0)
    row, shift_z = place
    key = row, (cell + shift_z) % cells
    sums[key] = sums[key] + part if key in sums else part


def close_transposed(sums, cells):
    return {
        row: jnp.concatenate(
            [jnp.sum(sums[row, cell], axis=0, keepdims=True) for cell in range(cells)], axis=0
        )
        for row in ROWS
    }


def transposed_products(tiles_ref, value):
    cells = value.shape[0]
    columns = columns_of(value)
    sums = {}
    for cell in range(cells):
        for slot, (place, _) in enumerate(reached_cells(cells)):
            add_transposed(sums, place, cell, cells, tiles_ref[slot, cell], columns[cell])
    return close_transposed(sums, cells)


def direct_products(tiles_ref, rows):
    cells = rows[0, 0].shape[0]
    found = []
    for cell in range(cells):
        total = None
        for slot, ((row, shift_z), _) in enumerate(reached_cells(cells)):
            reached = (cell + shift_z) % cells
            product = tiles_ref[slot, cell] * rows[row][reached : reached + 1]
            total = product if total is None else total + product
        found.append(jnp.sum(total.T, axis=0, keepdims=True))
    return jnp.concatenate(found, axis=0)


def put_rows(grid, send_ref, sent, value):
    cells = value.shape[0]
    ahead, behind = neighbours(grid)
    for place, row in enumerate(AHEAD):
        send_ref[ahead[place], :cells, :] = sent[row]
        send_ref[behind[place], :cells, :] = value


def turned(value, shift, axis):
    size = value.shape[axis]
    shift %= size
    if shift == 0:
        return value
    return jnp.concatenate(
        [lax.slice_in_dim(value, shift, size, axis=axis), lax.slice_in_dim(value, 0, shift, axis=axis)],
        axis=axis,
    )


def lanes_of(left, right):
    return jnp.sum(left * right, axis=0, keepdims=True)


def whole(lanes):
    return jnp.sum(lanes, axis=1, keepdims=True)


def applied(grid, tiles_ref, received_ref, value, own, diagonal, occupied):
    cells = value.shape[0]
    ahead, behind = neighbours(grid)
    rows = {(0, 0): value}
    total = diagonal * value + own
    for place, row in enumerate(AHEAD):
        rows[row] = received_ref[ahead[place], :cells, :]
        total = total + received_ref[behind[place], :cells, :]
    return occupied * (total + direct_products(tiles_ref, rows))


def start_kernel(
    grid, tiles_hbm, chi_hbm, species_hbm, counts_hbm, hardness_hbm,
    send_ref, own_ref, residual_ref, diagonal_ref, occupied_ref, tiles_ref,
    chi_ref, species_ref, counts_ref, hardness_ref, more_ref, small_sem, kept_sem, more_sem,
):
    cells, slots = chi_ref.shape
    places = reached_cells(cells)
    small = [
        pltpu.make_async_copy(source, target, small_sem.at[index])
        for index, (source, target) in enumerate(
            (
                (chi_hbm, chi_ref),
                (counts_hbm, counts_ref),
                (species_hbm, species_ref),
                (hardness_hbm, hardness_ref),
            )
        )
    ]
    for copy in small:
        copy.start()
    copies, spare = [], 0
    for slot, (_, offsets) in enumerate(places):
        group = [pltpu.make_async_copy(tiles_hbm.at[offsets[0]], tiles_ref.at[slot], kept_sem.at[slot])]
        for offset in offsets[1:]:
            group.append(
                pltpu.make_async_copy(tiles_hbm.at[offset], more_ref.at[spare], more_sem.at[spare])
            )
            spare += 1
        for copy in group:
            copy.start()
        copies.append(group)

    for copy in small:
        copy.wait()
    slot_ids = lax.broadcasted_iota(jnp.int32, (cells, slots), 1)
    cell_ids = lax.broadcasted_iota(jnp.int32, (cells, slots), 0)
    filled = jnp.zeros((cells, slots), jnp.int32)
    for cell in range(cells):
        filled = jnp.where(cell_ids == cell, counts_ref[cell], filled)
    occupied = jnp.where(slot_ids < filled, 1.0, 0.0)
    residual = -chi_ref[...] * occupied
    species = species_ref[...]
    diagonal = jnp.zeros_like(residual)
    for element in range(hardness_ref.shape[0]):
        diagonal = diagonal + jnp.where(species == element, hardness_ref[element], 0.0)
    occupied_ref[...] = occupied
    residual_ref[...] = residual
    diagonal_ref[...] = diagonal
    columns = columns_of(residual)

    sums, spare = {}, 0
    for slot, (place, offsets) in enumerate(places):
        for copy in copies[slot]:
            copy.wait()
        for cell in range(cells):
            tile = tiles_ref[slot, cell]
            for extra in range(len(offsets) - 1):
                tile = tile + more_ref[spare + extra, cell]
            if len(offsets) > 1:
                tiles_ref[slot, cell] = tile
            add_transposed(sums, place, cell, cells, tile, columns[cell])
        spare += len(offsets) - 1
    sent = close_transposed(sums, cells)
    put_rows(grid, send_ref, sent, residual)
    own_ref[...] = sent[0, 0]


def first_kernel(
    grid, tiles_ref, received_ref, residual_ref, own_ref, diagonal_ref, occupied_ref,
    send_ref, next_own_ref, image_ref,
):
    residual = residual_ref[...]
    cells = residual.shape[0]
    image = applied(
        grid, tiles_ref, received_ref, residual, own_ref[...], diagonal_ref[...], occupied_ref[...]
    )
    image_ref[...] = image
    parts = jnp.concatenate([lanes_of(residual, residual), lanes_of(residual, image)], axis=0)
    sent = transposed_products(tiles_ref, image)
    next_own_ref[...] = sent[0, 0]
    count = send_ref.shape[0]
    send_ref[:, cells : cells + 2, :] = jnp.broadcast_to(parts[None], (count,) + parts.shape)
    put_rows(grid, send_ref, sent, image)


def second_kernel(
    grid, tiles_ref, received_ref, residual_ref, image_ref, own_ref, diagonal_ref, occupied_ref,
    send_ref, next_own_ref, state_ref, sums_ref,
):
    r0, w = residual_ref[...], image_ref[...]
    cells, slots = r0.shape
    diagonal = diagonal_ref[...]
    aw = applied(grid, tiles_ref, received_ref, w, own_ref[...], diagonal, occupied_ref[...])
    totals = whole(jnp.sum(received_ref[:, cells : cells + 2, :], axis=0))
    norm, curvature = totals[0:1], totals[1:2]
    step = norm / curvature
    r = r0 - step * w
    ar = w - step * aw
    v = r - step * ar
    sent = transposed_products(tiles_ref, v)
    next_own_ref[...] = sent[0, 0]
    for index, value in enumerate((aw, r, ar, v)):
        state_ref[index] = value
    sums_ref[0:1] = jnp.broadcast_to(norm, (1, slots))
    sums_ref[1:2] = jnp.broadcast_to(curvature, (1, slots))

    pairs = {
        "vv": (v, v), "vr": (v, r), "vw": (v, w), "rr": (r, r), "rw": (r, w), "ww": (w, w),
        "vAv": (v, diagonal * v + 2.0 * sent[0, 0]), "vAr": (v, ar), "vAw": (v, aw),
        "rAr": (r, ar), "rAw": (r, aw), "wAw": (w, aw),
    }
    width = slots // FOLD
    lane = lax.broadcasted_iota(jnp.int32, (FOLD, slots), 1) // width
    line = lax.broadcasted_iota(jnp.int32, (FOLD, slots), 0)
    packed = []
    for first in range(0, cells * FOLD, FOLD):
        names = SUMS[first : first + FOLD]
        parts = [lanes_of(*pairs[name]) for name in names]
        parts += [jnp.zeros((1, slots), jnp.float32)] * (FOLD - len(names))
        block = jnp.concatenate(parts, axis=0)
        shift = slots // 2
        while shift >= width:
            block = block + pltpu.roll(block, shift, 1)
            shift //= 2
        packed.append(jnp.sum(jnp.where(lane == line, block, 0.0), axis=0, keepdims=True))
    message = [sent[row] for row in AHEAD] + [v, jnp.concatenate(packed, axis=0)]
    count = send_ref.shape[0]
    for index, part in enumerate(message):
        send_ref[:, index] = jnp.broadcast_to(part[None], (count,) + part.shape)


def last_kernel(
    grid, tiles_ref, received_ref, residual_ref, image_ref, state_ref, own_ref, diagonal_ref,
    occupied_ref, sums_ref, out_charges_ref, out_residual_ref,
):
    r0, w = residual_ref[...], image_ref[...]
    cells, slots = r0.shape
    aw, r, ar, v = (state_ref[index] for index in range(4))
    ahead, behind = neighbours(grid)
    at_value = len(AHEAD)

    everywhere = received_ref[:, at_value].reshape(grid + (cells, slots))
    crossed = None
    for place, (shift_x, shift_y) in enumerate(AHEAD):
        sent = received_ref[:, place].reshape(grid + (cells, slots))
        reached = turned(turned(everywhere, shift_x, 0), shift_y, 1)
        product = sent * reached
        crossed = product if crossed is None else crossed + product
    crossed = whole(jnp.sum(jnp.sum(crossed, axis=(0, 1)), axis=0, keepdims=True))
    parts = jnp.sum(received_ref[:, at_value + 1], axis=0)
    lane = lax.broadcasted_iota(jnp.int32, (1, slots), 1) // (slots // FOLD)
    total = {}
    for index, name in enumerate(SUMS):
        line = index // FOLD
        total[name] = whole(jnp.where(lane == index % FOLD, parts[line : line + 1], 0.0))
    total["vAv"] = total["vAv"] + 2.0 * crossed

    rows = {(0, 0): v}
    av = diagonal_ref[...] * v + own_ref[...]
    for place, row in enumerate(AHEAD):
        rows[row] = received_ref[ahead[place], at_value]
        av = av + received_ref[behind[place], place]
    av = occupied_ref[...] * (av + direct_products(tiles_ref, rows))

    norm0, curvature0 = sums_ref[0:1, 0:1], sums_ref[1:2, 0:1]
    step0 = norm0 / curvature0
    norm1 = total["rr"]
    ratio1 = norm1 / norm0
    curvature1 = total["rAr"] - ratio1 * ratio1 * curvature0
    step1 = norm1 / curvature1
    one = step1 / step0
    two = 1.0 - one
    three = -step1 * ratio1

    def form(vv, vr, vw, rr, rw, ww):
        return (
            one * one * total[vv] + two * two * total[rr] + three * three * total[ww]
            + 2.0 * (one * two * total[vr] + one * three * total[vw] + two * three * total[rw])
        )

    norm2 = form("vv", "vr", "vw", "rr", "rw", "ww")
    product2 = form("vAv", "vAr", "vAw", "rAr", "rAw", "wAw")
    ratio2 = norm2 / norm1
    curvature2 = product2 - ratio2 * ratio2 * curvature1
    step2 = norm2 / curvature2
    residual2 = one * v + two * r + three * w
    image2 = one * av + two * ar + three * aw
    direction1 = r + ratio1 * r0
    push1 = ar + ratio1 * w
    direction2 = residual2 + ratio2 * direction1
    push2 = image2 + ratio2 * push1
    out_charges_ref[...] = step0 * r0 + step1 * direction1 + step2 * direction2
    out_residual_ref[...] = residual2 - step2 * push2


def body(tiles, chi, species, counts, hardness):
    grid = lax.axis_size("gx"), lax.axis_size("gy")
    count = grid[0] * grid[1]
    own_tiles = tiles[:, 0, 0]
    offsets = own_tiles.shape[0]
    cells, slots = chi.shape[2:]
    places = len(reached_cells(cells))
    vmem = pl.BlockSpec(memory_space=pltpu.VMEM)
    hbm = pl.BlockSpec(memory_space=pltpu.HBM)

    def shape(*sizes):
        return jax.ShapeDtypeStruct(sizes, jnp.float32)

    value = shape(cells, slots)

    def call(kernel, outputs, specs, scratch=()):
        return pl.pallas_call(
            kernel,
            out_shape=outputs,
            in_specs=specs,
            out_specs=[vmem] * len(outputs),
            scratch_shapes=scratch,
            compiler_params=pltpu.CompilerParams(vmem_limit_bytes=24 * 2**20),
        )

    def exchange(buffer):
        return lax.all_to_all(buffer, ("gx", "gy"), 0, 0, tiled=True)

    send, own, r0, diagonal, occupied, kept = call(
        functools.partial(start_kernel, grid),
        (shape(count, cells, slots), value, value, value, value, shape(places, cells, slots, slots)),
        [hbm] * 5,
        (
            pltpu.VMEM((cells, slots), jnp.float32),
            pltpu.VMEM((cells, slots), jnp.int32),
            pltpu.SMEM((cells,), jnp.int32),
            pltpu.SMEM(hardness.shape, jnp.float32),
            pltpu.VMEM((max(offsets - places, 1), cells, slots, slots), jnp.float32),
            pltpu.SemaphoreType.DMA((4,)),
            pltpu.SemaphoreType.DMA((places,)),
            pltpu.SemaphoreType.DMA((max(offsets - places, 1),)),
        ),
    )(own_tiles, chi[0, 0], species[0, 0], counts[0, 0], hardness)
    received = exchange(send)
    send, own, w = call(
        functools.partial(first_kernel, grid),
        (shape(count, cells + 2, slots), value, value),
        [vmem] * 6,
    )(kept, received, r0, own, diagonal, occupied)
    received = exchange(send)
    send, own, state, sums = call(
        functools.partial(second_kernel, grid),
        (shape(count, len(AHEAD) + 2, cells, slots), value, shape(4, cells, slots), shape(2, slots)),
        [vmem] * 7,
    )(kept, received, r0, w, own, diagonal, occupied)
    received = exchange(send)
    charges, residual = call(
        functools.partial(last_kernel, grid), (value, value), [vmem] * 9
    )(kept, received, r0, w, state, own, diagonal, occupied, sums)
    return charges[None, None], residual[None, None]


def solution(mesh):
    in_specs = (
        P(None, "gx", "gy", None, None, None),
        P("gx", "gy", None, None),
        P("gx", "gy", None, None),
        P("gx", "gy", None),
        P(),
    )
    out_specs = (P("gx", "gy", None, None), P("gx", "gy", None, None))
    return jax.shard_map(body, mesh=mesh, in_specs=in_specs, out_specs=out_specs, check_vma=False)
```

time: 268 us -> 48.9 us (0.18)
  blocking collectives: 200 us -> 36.6 us
  starting transfers between devices: 32.5 us -> 0 us
  matrix products: 12.7 us -> 0 us
  other arithmetic: 9.34 us -> 0 us
  between operations: 7.87 us -> 0.67 us
  Pallas kernels: 0 us -> 6.89 us
  local copies, waits for them, and re-layouts: 1.04 us -> 4.51 us
  waiting for transfers between devices: 3.16 us -> 0 us
    psum x5 -> x0, blocking collectives: 200 us -> none  [inner_sums(): return lax.psum(partial_value, ('gx', 'gy'))]
    all_to_all x0 -> x3, blocking collectives: none -> 36.6 us  [exchange(): return lax.all_to_all(buffer, ('gx', 'gy'), 0, 0, tiled=True)]
    ppermute x24 -> x0, starting transfers between devices: 32.5 us -> none  [the longest x18 26.5 us: shifted(): return lax.ppermute(value, axis, pairs)]
    dot_general x6 -> x0, matrix products: 12.7 us -> none  [the longest x3 8 us: apply_half(): summed = jnp.einsum('kzab,kzb->za', own_tiles, fronts, precision=exact_mode)]
    pallas_call x0 -> x4, Pallas kernels: none -> 6.89 us  [the longest x1 4.63 us: body(): call(functools.partial(start_kernel, grid), (shape(count, cells, slots),...]
    reduce_sum x5 -> x0, other arithmetic: 6.05 us -> none  [the longest x3 4.71 us: body(): step_size = norm_now / inner_sums(jnp.sum(direction * applied))]
    unnamed x34 -> x10, local copies, waits for them, and re-layouts: 0.23 us -> 4.51 us
    ppermute x24 -> x0, waiting for transfers between devices: 3.16 us -> none  [the longest x18 3.15 us: shifted(): return lax.ppermute(value, axis, pairs)]
  transfers between devices with their start and end apart: 24 -> 0, of which waited for: 3 -> 0; matrix products, arithmetic and copies ran while one was open for 6% -> 0% of each run, Pallas kernels for 0% -> 0%
where the time goes in v2:
time: 48.9 us; the launch traced here: 48.7 us
  blocking collectives  36.6 us (75%)
  Pallas kernels  6.89 us (14%)
  local copies, waits for them, and re-layouts  4.51 us (9%)
  between operations  0.67 us (1%)
    all_to_all x3, blocking collectives, exchange(): return lax.all_to_all(buffer, ('gx', 'gy'), 0, 0, tiled=True)  36.6 us
    pallas_call x1, Pallas kernels, body(): call(functools.partial(start_kernel, grid), (shape(count, cells, slots),...  4.63 us
    unnamed x10, local copies, waits for them, and re-layouts  4.51 us

profile of v2, /device:TPU:0, one launch (start us, length us, event | category | flops | bytes accessed | tf_op | source)
XLA Modules:
  0.0 48.7 jit_solution(9642092454777986997)
XLA Ops:
  0.6 0.0 copy-start
  0.6 1.8 %copy-done = f32[23,1,1,2,128,128]{5,4,3,2,1,0:T(8,128)S(1)} copy-done((f32[23,1,1,2,128,128]{5,4,3,2,1,0:T(8,128)S(1)}, f32[23,1,1,2,128,128]{5,4,3,2,1,0:T(8,128)}, u32[]{:S(2)}) %copy-start) | copy-done | bytes 3014680
  2.5 0.0 copy-start.1
  2.5 0.7 %copy-done.1 = f32[1,1,2,128]{3,2,1,0:T(2,128)S(1)} copy-done((f32[1,1,2,128]{3,2,1,0:T(2,128)S(1)}, f32[1,1,2,128]{3,2,1,0:T(2,128)}, u32[]{:S(2)}) %copy-start.1) | copy-done | bytes 1048
  3.2 0.0 copy-start.2
  3.2 0.7 %copy-done.2 = s32[1,1,2,128]{3,2,1,0:T(2,128)S(1)} copy-done((s32[1,1,2,128]{3,2,1,0:T(2,128)S(1)}, s32[1,1,2,128]{3,2,1,0:T(2,128)}, u32[]{:S(2)}) %copy-start.2) | copy-done | bytes 1048
  3.8 0.0 copy-start.3
  3.8 0.7 %copy-done.3 = s32[1,1,2]{2,1,0:T(1,128)S(1)} copy-done((s32[1,1,2]{2,1,0:T(1,128)S(1)}, s32[1,1,2]{2,1,0:T(1,128)}, u32[]{:S(2)}) %copy-start.3) | copy-done | bytes 32
  4.5 0.0 copy-start.4
  4.5 0.7 %copy-done.4 = f32[4]{0:T(128)S(1)} copy-done((f32[4]{0:T(128)S(1)}, f32[4]{0:T(128)}, u32[]{:S(2)}) %copy-start.4) | copy-done | bytes 40
  5.2 4.6 %shard_map.68 = (f32[32,2,128]{2,1,0:T(2,128)S(1)}, f32[2,128]{1,0:T(2,128)S(1)}, f32[2,128]{1,0:T(2,128)S(1)}, f32[2,128]{1,0:T(2,128)S(1)}, f32[2,128]{1,0:T(2,128)S(1)}, /*index=5*/f32[16,2,128,128]{3,2,1,0:T(8,128)S(1)}) custom-call(f32[23,2,128,128]{3,2,1,0:T(8,128)S(1)} %bitcast.6, f32[2,128]{1,0:T(2,128)S(1)} %bitcast.7, s32[2,128]{1,0:T(2,128)S(1)} %bitcast.8, ...), custom_call_target="tpu_custom_call" | custom-call | tf_op jit(solution)/shard_map/pallas_call | solution.py:353
  9.8 14.4 %all_to_all.15.received_ref = f32[32,2,128]{2,1,0:T(2,128)S(1)} all-to-all(f32[32,2,128]{2,1,0:T(2,128)S(1)} %get-tuple-element.18), channel_id=1, replica_groups=mesh['gx'=8,'gy'=4] {'gx','gy'}, dimensions={0} | all-to-all | bytes 65536 | tf_op jit(solution)/shard_map/all_to_all | solution.py:351
  24.2 0.5 shard_map.69
  24.7 9.1 %all_to_all.16.received_ref = f32[32,4,128]{2,1,0:T(4,128)S(1)} all-to-all(f32[32,4,128]{2,1,0:T(4,128)S(1)} %get-tuple-element.23), channel_id=1, replica_groups=mesh['gx'=8,'gy'=4] {'gx','gy'}, dimensions={0} | all-to-all | bytes 131072 | tf_op jit(solution)/shard_map/all_to_all | solution.py:351
  33.8 0.8 %shard_map.70 = (f32[32,9,2,128]{3,2,1,0:T(2,128)S(1)}, f32[2,128]{1,0:T(2,128)S(1)}, f32[4,2,128]{2,1,0:T(2,128)S(1)}, f32[2,128]{1,0:T(2,128)S(1)}) custom-call(f32[16,2,128,128]{3,2,1,0:T(8,128)S(1)} %get-tuple-element.17.tiles_ref, f32[32,4,128]{2,1,0:T(4,128)S(1)} %all_to_all.16.received_ref, f32[2,128]{1,0:T(2,128)S(1)} %get-tuple-element.19.residual_ref, ...), custom_call_target="tpu_custom_call" | custom-call | tf_op jit(solution)/shard_map/pallas_call | solution.py:375
  34.6 13.1 %all_to_all.17.received_ref = f32[32,9,2,128]{3,2,1,0:T(2,128)S(1)} all-to-all(f32[32,9,2,128]{3,2,1,0:T(2,128)S(1)} %get-tuple-element.26), channel_id=1, replica_groups=mesh['gx'=8,'gy'=4] {'gx','gy'}, dimensions={0} | all-to-all | bytes 589824 | tf_op jit(solution)/shard_map/all_to_all | solution.py:351
  47.7 1.0 %shard_map.71 = (f32[2,128]{1,0:T(2,128)}, f32[2,128]{1,0:T(2,128)}) custom-call(f32[16,2,128,128]{3,2,1,0:T(8,128)S(1)} %get-tuple-element.17.tiles_ref, f32[32,9,2,128]{3,2,1,0:T(2,128)S(1)} %all_to_all.17.received_ref, f32[2,128]{1,0:T(2,128)S(1)} %get-tuple-element.19.residual_ref, f32[2,128]{1,0:T(2,128)S(1)} %get-tuple-element.24.image_ref, ...), custom_call_target="tpu_custom_call" | custom-call | tf_op jit(solution)/shard_map/pallas_call | solution.py:381
Async XLA Ops:
  0.6 1.9 %copy-start = (f32[23,1,1,2,128,128]{5,4,3,2,1,0:T(8,128)S(1)}, f32[23,1,1,2,128,128]{5,4,3,2,1,0:T(8,128)}, u32[]{:S(2)}) copy-start(f32[23,1,1,2,128,128]{5,4,3,2,1,0:T(8,128)} %param.5) | copy-start | bytes 9043972
  2.5 0.7 %copy-start.1 = (f32[1,1,2,128]{3,2,1,0:T(2,128)S(1)}, f32[1,1,2,128]{3,2,1,0:T(2,128)}, u32[]{:S(2)}) copy-start(f32[1,1,2,128]{3,2,1,0:T(2,128)} %param.6) | copy-start | bytes 3076
  3.2 0.7 %copy-start.2 = (s32[1,1,2,128]{3,2,1,0:T(2,128)S(1)}, s32[1,1,2,128]{3,2,1,0:T(2,128)}, u32[]{:S(2)}) copy-start(s32[1,1,2,128]{3,2,1,0:T(2,128)} %param.7) | copy-start | bytes 3076
  3.8 0.7 %copy-start.3 = (s32[1,1,2]{2,1,0:T(1,128)S(1)}, s32[1,1,2]{2,1,0:T(1,128)}, u32[]{:S(2)}) copy-start(s32[1,1,2]{2,1,0:T(1,128)} %param.8) | copy-start | bytes 28
  4.5 0.7 %copy-start.4 = (f32[4]{0:T(128)S(1)}, f32[4]{0:T(128)}, u32[]{:S(2)}) copy-start(f32[4]{0:T(128)} %hardness_hbm.1) | copy-start | bytes 52

commit v3 on v2

--- a/solution.py
+++ b/solution.py
@@ -350,6 +350,8 @@
     def exchange(buffer):
         return lax.all_to_all(buffer, ("gx", "gy"), 0, 0, tiled=True)
 
+    arguments = (own_tiles, chi[0, 0], species[0, 0], counts[0, 0], hardness)
+    arguments = [pltpu.with_memory_space_constraint(each, pltpu.HBM) for each in arguments]
     send, own, r0, diagonal, occupied, kept = call(
         functools.partial(start_kernel, grid),
         (shape(count, cells, slots), value, value, value, value, shape(places, cells, slots, slots)),
@@ -364,7 +366,7 @@
             pltpu.SemaphoreType.DMA((places,)),
             pltpu.SemaphoreType.DMA((max(offsets - places, 1),)),
         ),
-    )(own_tiles, chi[0, 0], species[0, 0], counts[0, 0], hardness)
+    )(*arguments)
     received = exchange(send)
     send, own, w = call(
         functools.partial(first_kernel, grid),

time: 48.9 us -> 42 us (0.86)
  local copies, waits for them, and re-layouts: 4.51 us -> 0 us
  Pallas kernels: 6.89 us -> 4.54 us
    unnamed x10 -> x0, local copies, waits for them, and re-layouts: 4.51 us -> none
    pallas_call x1, Pallas kernels: 4.63 us -> 2.28 us  [body(): call(functools.partial(start_kernel, grid), (shape(count, cells, slots),...]
where the time goes in v3:
time: 42 us; the launch traced here: 41.8 us
  blocking collectives  36.6 us (87%)
  Pallas kernels  4.54 us (11%)
  between operations  0.66 us (2%)
    all_to_all x3, blocking collectives, exchange(): return lax.all_to_all(buffer, ('gx', 'gy'), 0, 0, tiled=True)  36.6 us
    pallas_call x1, Pallas kernels, body(): call(functools.partial(start_kernel, grid), (shape(count, cells, slots),...  2.28 us
    pallas_call x1, Pallas kernels, body(): call(functools.partial(last_kernel, grid), (value, value), [vmem] * 9)  0.95 us

profile of v3, /device:TPU:0, one launch (start us, length us, event | category | flops | bytes accessed | tf_op | source)
XLA Modules:
  0.0 41.8 jit_solution(3088929280039554230)
XLA Ops:
  0.6 2.3 %shard_map.68 = (f32[32,2,128]{2,1,0:T(2,128)S(1)}, f32[2,128]{1,0:T(2,128)S(1)}, f32[2,128]{1,0:T(2,128)S(1)}, f32[2,128]{1,0:T(2,128)S(1)}, f32[2,128]{1,0:T(2,128)S(1)}, /*index=5*/f32[16,2,128,128]{3,2,1,0:T(8,128)S(1)}) custom-call(f32[23,2,128,128]{3,2,1,0:T(8,128)} %bitcast.6, f32[2,128]{1,0:T(2,128)} %bitcast.7, s32[2,128]{1,0:T(2,128)} %bitcast.8, ...), custom_call_target="tpu_custom_call" | custom-call | tf_op jit(solution)/shard_map/pallas_call | solution.py:355
  2.9 14.4 %all_to_all.15.received_ref = f32[32,2,128]{2,1,0:T(2,128)S(1)} all-to-all(f32[32,2,128]{2,1,0:T(2,128)S(1)} %get-tuple-element.18), channel_id=1, replica_groups=mesh['gx'=8,'gy'=4] {'gx','gy'}, dimensions={0} | all-to-all | bytes 65536 | tf_op jit(solution)/shard_map/all_to_all | solution.py:351
  17.3 0.5 %shard_map.69 = (f32[32,4,128]{2,1,0:T(4,128)S(1)}, f32[2,128]{1,0:T(2,128)S(1)}, f32[2,128]{1,0:T(2,128)S(1)}) custom-call(f32[16,2,128,128]{3,2,1,0:T(8,128)S(1)} %get-tuple-element.17.tiles_ref, f32[32,2,128]{2,1,0:T(2,128)S(1)} %all_to_all.15.received_ref, f32[2,128]{1,0:T(2,128)S(1)} %get-tuple-element.19.residual_ref, ...), custom_call_target="tpu_custom_call" | custom-call | tf_op jit(solution)/shard_map/pallas_call | solution.py:371
  17.8 9.1 %all_to_all.16.received_ref = f32[32,4,128]{2,1,0:T(4,128)S(1)} all-to-all(f32[32,4,128]{2,1,0:T(4,128)S(1)} %get-tuple-element.23), channel_id=1, replica_groups=mesh['gx'=8,'gy'=4] {'gx','gy'}, dimensions={0} | all-to-all | bytes 131072 | tf_op jit(solution)/shard_map/all_to_all | solution.py:351
  26.9 0.8 %shard_map.70 = (f32[32,9,2,128]{3,2,1,0:T(2,128)S(1)}, f32[2,128]{1,0:T(2,128)S(1)}, f32[4,2,128]{2,1,0:T(2,128)S(1)}, f32[2,128]{1,0:T(2,128)S(1)}) custom-call(f32[16,2,128,128]{3,2,1,0:T(8,128)S(1)} %get-tuple-element.17.tiles_ref, f32[32,4,128]{2,1,0:T(4,128)S(1)} %all_to_all.16.received_ref, f32[2,128]{1,0:T(2,128)S(1)} %get-tuple-element.19.residual_ref, ...), custom_call_target="tpu_custom_call" | custom-call | tf_op jit(solution)/shard_map/pallas_call | solution.py:377
  27.7 13.1 %all_to_all.17.received_ref = f32[32,9,2,128]{3,2,1,0:T(2,128)S(1)} all-to-all(f32[32,9,2,128]{3,2,1,0:T(2,128)S(1)} %get-tuple-element.26), channel_id=1, replica_groups=mesh['gx'=8,'gy'=4] {'gx','gy'}, dimensions={0} | all-to-all | bytes 589824 | tf_op jit(solution)/shard_map/all_to_all | solution.py:351
  40.8 1.0 %shard_map.71 = (f32[2,128]{1,0:T(2,128)}, f32[2,128]{1,0:T(2,128)}) custom-call(f32[16,2,128,128]{3,2,1,0:T(8,128)S(1)} %get-tuple-element.17.tiles_ref, f32[32,9,2,128]{3,2,1,0:T(2,128)S(1)} %all_to_all.17.received_ref, f32[2,128]{1,0:T(2,128)S(1)} %get-tuple-element.19.residual_ref, f32[2,128]{1,0:T(2,128)S(1)} %get-tuple-element.24.image_ref, ...), custom_call_target="tpu_custom_call" | custom-call | tf_op jit(solution)/shard_map/pallas_call | solution.py:383

commit v4 on v3

--- a/solution.py
+++ b/solution.py
@@ -10,7 +10,7 @@
 AHEAD = ((0, 1), (1, -1), (1, 0), (1, 1), (2, -1), (2, 0), (2, 1))
 ROWS = ((0, 0),) + AHEAD
 SUMS = ("vv", "vr", "vw", "rr", "rw", "ww", "vAv", "vAr", "vAw", "rAr", "rAw", "wAw")
-FOLD = 8
+FOLD = 16
 
 
 def forward_offsets():
@@ -241,55 +241,76 @@
     width = slots // FOLD
     lane = lax.broadcasted_iota(jnp.int32, (FOLD, slots), 1) // width
     line = lax.broadcasted_iota(jnp.int32, (FOLD, slots), 0)
-    packed = []
-    for first in range(0, cells * FOLD, FOLD):
-        names = SUMS[first : first + FOLD]
-        parts = [lanes_of(*pairs[name]) for name in names]
-        parts += [jnp.zeros((1, slots), jnp.float32)] * (FOLD - len(names))
-        block = jnp.concatenate(parts, axis=0)
-        shift = slots // 2
-        while shift >= width:
-            block = block + pltpu.roll(block, shift, 1)
-            shift //= 2
-        packed.append(jnp.sum(jnp.where(lane == line, block, 0.0), axis=0, keepdims=True))
-    message = [sent[row] for row in AHEAD] + [v, jnp.concatenate(packed, axis=0)]
-    count = send_ref.shape[0]
-    for index, part in enumerate(message):
-        send_ref[:, index] = jnp.broadcast_to(part[None], (count,) + part.shape)
-
-
-def last_kernel(
-    grid, tiles_ref, received_ref, residual_ref, image_ref, state_ref, own_ref, diagonal_ref,
-    occupied_ref, sums_ref, out_charges_ref, out_residual_ref,
+    parts = [lanes_of(*pairs[name]) for name in SUMS]
+    parts += [jnp.zeros((1, slots), jnp.float32)] * (FOLD - len(SUMS))
+    block = jnp.concatenate(parts, axis=0)
+    shift = slots // 2
+    while shift >= width:
+        block = block + pltpu.roll(block, shift, 1)
+        shift //= 2
+    packed = jnp.sum(jnp.where(lane == line, block, 0.0), axis=0, keepdims=True)
+    half = cells // 2
+    message = [sent[row] for row in AHEAD] + [v]
+    for device in range(send_ref.shape[0]):
+        low = (device % 2) * half
+        for index, part in enumerate(message):
+            send_ref[device, index] = part[low : low + half]
+        send_ref[device, len(message) + 1, 0:1] = packed
+    ahead, behind = neighbours(grid)
+    for found, parts in ((ahead, message[:-1]), (behind, message[-1:] * len(AHEAD))):
+        for device, part in zip(found, parts):
+            other = jnp.where(lax.rem(device, 2) == 0, part[half:], part[:half])
+            send_ref[device, len(message)] = other
+
+
+def both_halves(mine, other):
+    first = lax.rem(lax.axis_index("gy"), 2) == 0
+    return jnp.concatenate(
+        [jnp.where(first, mine, other), jnp.where(first, other, mine)], axis=0
+    )
+
+
+def cross_kernel(grid, received_ref, crossed_ref, parts_ref):
+    half, slots = received_ref.shape[2:]
+    at_value = len(AHEAD)
+    everywhere = received_ref[:, at_value].reshape(grid + (half, slots))
+    crossed = None
+    for place, (shift_x, shift_y) in enumerate(AHEAD):
+        sent = received_ref[:, place].reshape(grid + (half, slots))
+        product = sent * turned(turned(everywhere, shift_x, 0), shift_y, 1)
+        crossed = product if crossed is None else crossed + product
+    crossed_ref[...] = jnp.sum(jnp.sum(crossed, axis=(0, 1)), axis=0, keepdims=True)
+    parts_ref[...] = jnp.sum(received_ref[:, at_value + 2, 0:1], axis=0)
+
+
+def image_kernel(
+    grid, tiles_ref, received_ref, state_ref, own_ref, diagonal_ref, occupied_ref, image_ref
 ):
-    r0, w = residual_ref[...], image_ref[...]
-    cells, slots = r0.shape
-    aw, r, ar, v = (state_ref[index] for index in range(4))
+    v = state_ref[3]
     ahead, behind = neighbours(grid)
     at_value = len(AHEAD)
-
-    everywhere = received_ref[:, at_value].reshape(grid + (cells, slots))
-    crossed = None
-    for place, (shift_x, shift_y) in enumerate(AHEAD):
-        sent = received_ref[:, place].reshape(grid + (cells, slots))
-        reached = turned(turned(everywhere, shift_x, 0), shift_y, 1)
-        product = sent * reached
-        crossed = product if crossed is None else crossed + product
-    crossed = whole(jnp.sum(jnp.sum(crossed, axis=(0, 1)), axis=0, keepdims=True))
-    parts = jnp.sum(received_ref[:, at_value + 1], axis=0)
+    rows = {(0, 0): v}
+    image = diagonal_ref[...] * v + own_ref[...]
+    for place, row in enumerate(AHEAD):
+        front, back = ahead[place], behind[place]
+        rows[row] = both_halves(received_ref[front, at_value], received_ref[front, at_value + 1])
+        image = image + both_halves(received_ref[back, place], received_ref[back, at_value + 1])
+    image_ref[...] = occupied_ref[...] * (image + direct_products(tiles_ref, rows))
+
+
+def last_kernel(
+    residual_ref, first_image_ref, state_ref, image_ref, parts_ref, crossed_ref, mate_ref, sums_ref,
+    out_charges_ref, out_residual_ref,
+):
+    r0, w, av = residual_ref[...], first_image_ref[...], image_ref[...]
+    slots = r0.shape[1]
+    aw, r, ar, v = (state_ref[index] for index in range(4))
+    parts = parts_ref[...]
     lane = lax.broadcasted_iota(jnp.int32, (1, slots), 1) // (slots // FOLD)
-    total = {}
-    for index, name in enumerate(SUMS):
-        line = index // FOLD
-        total[name] = whole(jnp.where(lane == index % FOLD, parts[line : line + 1], 0.0))
-    total["vAv"] = total["vAv"] + 2.0 * crossed
-
-    rows = {(0, 0): v}
-    av = diagonal_ref[...] * v + own_ref[...]
-    for place, row in enumerate(AHEAD):
-        rows[row] = received_ref[ahead[place], at_value]
-        av = av + received_ref[behind[place], place]
-    av = occupied_ref[...] * (av + direct_products(tiles_ref, rows))
+    total = {
+        name: whole(jnp.where(lane == index, parts, 0.0)) for index, name in enumerate(SUMS)
+    }
+    total["vAv"] = total["vAv"] + 2.0 * whole(crossed_ref[...] + mate_ref[...])
 
     norm0, curvature0 = sums_ref[0:1, 0:1], sums_ref[1:2, 0:1]
     step0 = norm0 / curvature0
@@ -328,6 +349,7 @@
     own_tiles = tiles[:, 0, 0]
     offsets = own_tiles.shape[0]
     cells, slots = chi.shape[2:]
+    assert cells % 2 == 0 and grid[1] % 2 == 0
     places = len(reached_cells(cells))
     vmem = pl.BlockSpec(memory_space=pltpu.VMEM)
     hbm = pl.BlockSpec(memory_space=pltpu.HBM)
@@ -376,13 +398,20 @@
     received = exchange(send)
     send, own, state, sums = call(
         functools.partial(second_kernel, grid),
-        (shape(count, len(AHEAD) + 2, cells, slots), value, shape(4, cells, slots), shape(2, slots)),
+        (shape(count, len(AHEAD) + 3, cells // 2, slots), value, shape(4, cells, slots), shape(2, slots)),
         [vmem] * 7,
     )(kept, received, r0, w, own, diagonal, occupied)
     received = exchange(send)
-    charges, residual = call(
-        functools.partial(last_kernel, grid), (value, value), [vmem] * 9
-    )(kept, received, r0, w, state, own, diagonal, occupied, sums)
+    crossed, parts = call(
+        functools.partial(cross_kernel, grid), (shape(1, slots), shape(1, slots)), [vmem]
+    )(received)
+    mate = lax.ppermute(crossed, "gy", [(place, place ^ 1) for place in range(grid[1])])
+    (image,) = call(functools.partial(image_kernel, grid), (value,), [vmem] * 6)(
+        kept, received, state, own, diagonal, occupied
+    )
+    charges, residual = call(last_kernel, (value, value), [vmem] * 8)(
+        r0, w, state, image, parts, crossed, mate, sums
+    )
     return charges[None, None], residual[None, None]
 
 

time: 42 us -> 40.4 us (0.962)
  blocking collectives: 36.6 us -> 33.8 us
  waiting for transfers between devices: 0 us -> 0.62 us
    all_to_all x3, blocking collectives: 36.6 us -> 33.8 us  [exchange(): return lax.all_to_all(buffer, ('gx', 'gy'), 0, 0, tiled=True)]
    ppermute x0 -> x1, waiting for transfers between devices: none -> 0.62 us  [body(): lax.ppermute(crossed, 'gy', [(place, place ^ 1) for place in range(grid[1...]
    pallas_call x2 -> x4, Pallas kernels: 1.78 us -> 1.93 us  [the longest x1 0.85 us: body(): call(functools.partial(second_kernel, grid), (shape(count, len(AHEAD) + 3...]
  transfers between devices with their start and end apart: 0 -> 1, of which waited for: 0 -> 1; matrix products, arithmetic and copies ran while one was open for 0% -> 0% of each run, Pallas kernels for 0% -> 1%
where the time goes in v4:
time: 40.4 us; the launch traced here: 40.2 us
  blocking collectives  33.8 us (84%)
  Pallas kernels  4.69 us (12%)
  between operations  0.66 us (2%)
  waiting for transfers between devices  0.62 us (2%)
    all_to_all x3, blocking collectives, exchange(): return lax.all_to_all(buffer, ('gx', 'gy'), 0, 0, tiled=True)  33.8 us
    pallas_call x1, Pallas kernels, body(): call(functools.partial(start_kernel, grid), (shape(count, cells, slots),...  2.28 us
    pallas_call x1, Pallas kernels, body(): call(functools.partial(second_kernel, grid), (shape(count, len(AHEAD) + 3...  0.85 us
  transfers between devices with their start and end apart: 1, of which 1 were waited for; matrix products, arithmetic and copies ran while one was open for 0% of the time, Pallas kernels for 1%

profile of v4, /device:TPU:0, one launch (start us, length us, event | category | flops | bytes accessed | tf_op | source)
XLA Modules:
  0.0 40.2 jit_solution(822847663382581612)
XLA Ops:
  0.6 2.3 %shard_map.68 = (f32[32,2,128]{2,1,0:T(2,128)S(1)}, f32[2,128]{1,0:T(2,128)S(1)}, f32[2,128]{1,0:T(2,128)S(1)}, f32[2,128]{1,0:T(2,128)S(1)}, f32[2,128]{1,0:T(2,128)S(1)}, /*index=5*/f32[16,2,128,128]{3,2,1,0:T(8,128)S(1)}) custom-call(f32[23,2,128,128]{3,2,1,0:T(8,128)} %bitcast.6, f32[2,128]{1,0:T(2,128)} %bitcast.7, s32[2,128]{1,0:T(2,128)} %bitcast.8, ...), custom_call_target="tpu_custom_call" | custom-call | tf_op jit(solution)/shard_map/pallas_call | solution.py:377
  2.9 14.4 %all_to_all.15.received_ref = f32[32,2,128]{2,1,0:T(2,128)S(1)} all-to-all(f32[32,2,128]{2,1,0:T(2,128)S(1)} %get-tuple-element.21), channel_id=1, replica_groups=mesh['gx'=8,'gy'=4] {'gx','gy'}, dimensions={0} | all-to-all | bytes 65536 | tf_op jit(solution)/shard_map/all_to_all | solution.py:373
  17.3 0.5 %shard_map.69 = (f32[32,4,128]{2,1,0:T(4,128)S(1)}, f32[2,128]{1,0:T(2,128)S(1)}, f32[2,128]{1,0:T(2,128)S(1)}) custom-call(f32[16,2,128,128]{3,2,1,0:T(8,128)S(1)} %get-tuple-element.20.tiles_ref, f32[32,2,128]{2,1,0:T(2,128)S(1)} %all_to_all.15.received_ref, f32[2,128]{1,0:T(2,128)S(1)} %get-tuple-element.19.residual_ref, ...), custom_call_target="tpu_custom_call" | custom-call | tf_op jit(solution)/shard_map/pallas_call | solution.py:393
  17.8 9.1 %all_to_all.16.received_ref = f32[32,4,128]{2,1,0:T(4,128)S(1)} all-to-all(f32[32,4,128]{2,1,0:T(4,128)S(1)} %get-tuple-element.26), channel_id=1, replica_groups=mesh['gx'=8,'gy'=4] {'gx','gy'}, dimensions={0} | all-to-all | bytes 131072 | tf_op jit(solution)/shard_map/all_to_all | solution.py:373
  26.9 0.9 %shard_map.70 = (f32[32,10,1,128]{3,2,1,0:T(1,128)S(1)}, f32[2,128]{1,0:T(2,128)S(1)}, f32[4,2,128]{2,1,0:T(2,128)S(1)}, f32[2,128]{1,0:T(2,128)S(1)}) custom-call(f32[16,2,128,128]{3,2,1,0:T(8,128)S(1)} %get-tuple-element.20.tiles_ref, f32[32,4,128]{2,1,0:T(4,128)S(1)} %all_to_all.16.received_ref, f32[2,128]{1,0:T(2,128)S(1)} %get-tuple-element.19.residual_ref, ...), custom_call_target="tpu_custom_call" | custom-call | tf_op jit(solution)/shard_map/pallas_call | solution.py:399
  27.8 10.3 %all_to_all.17.received_ref = f32[32,10,1,128]{3,2,1,0:T(1,128)S(1)} all-to-all(f32[32,10,1,128]{3,2,1,0:T(1,128)S(1)} %get-tuple-element.29), channel_id=1, replica_groups=mesh['gx'=8,'gy'=4] {'gx','gy'}, dimensions={0} | all-to-all | bytes 327680 | tf_op jit(solution)/shard_map/all_to_all | solution.py:373
  38.1 0.1 shard_map.72
  38.2 0.4 collective-permute-start
  38.6 0.2 shard_map.71.image_ref
  38.8 0.6 %collective-permute-done.mate_ref = f32[1,128]{1,0:T(1,128)S(1)} collective-permute-done((f32[1,128]{1,0:T(1,128)S(1)}, f32[1,128]{1,0:T(1,128)S(1)}, u32[]{:S(2)}, u32[]{:S(2)}) %collective-permute-start) | collective-permute-done | bytes 544 | tf_op jit(solution)/shard_map/ppermute | solution.py:408
  39.5 0.7 %shard_map.73 = (f32[2,128]{1,0:T(2,128)}, f32[2,128]{1,0:T(2,128)}) custom-call(f32[2,128]{1,0:T(2,128)S(1)} %get-tuple-element.19.residual_ref, f32[2,128]{1,0:T(2,128)S(1)} %get-tuple-element.25.image_ref.first_image_ref, f32[4,2,128]{2,1,0:T(2,128)S(1)} %get-tuple-element.28.state_ref, f32[2,128]{1,0:T(2,128)S(1)} %shard_map.71.image_ref, ...), custom_call_target="tpu_custom_call" | custom-call | tf_op jit(solution)/shard_map/pallas_call | solution.py:412
Async XLA Ops:
  38.2 1.2 %collective-permute-start = (f32[1,128]{1,0:T(1,128)S(1)}, f32[1,128]{1,0:T(1,128)S(1)}, u32[]{:S(2)}, u32[]{:S(2)}) collective-permute-start(f32[1,128]{1,0:T(1,128)S(1)} %get-tuple-element.32.crossed_ref), channel_id=1, source_target_pairs={{0,1},{1,0},{2,3},{3,2},{4,5},{5,4},{6,7},{7,6},{8,9},{9,8},{10,11... | collective-permute-start | bytes 1544 | tf_op jit(solution)/shard_map/ppermute | solution.py:408

commit v5 on v4

--- a/solution.py
+++ b/solution.py
@@ -10,7 +10,7 @@
 AHEAD = ((0, 1), (1, -1), (1, 0), (1, 1), (2, -1), (2, 0), (2, 1))
 ROWS = ((0, 0),) + AHEAD
 SUMS = ("vv", "vr", "vw", "rr", "rw", "ww", "vAv", "vAr", "vAw", "rAr", "rAw", "wAw")
-FOLD = 16
+CHUNKS = ((0, 8), (8, 14), (14, 20), (20, 23))
 
 
 def forward_offsets():
@@ -71,8 +71,8 @@
     columns = columns_of(value)
     sums = {}
     for cell in range(cells):
-        for slot, (place, _) in enumerate(reached_cells(cells)):
-            add_transposed(sums, place, cell, cells, tiles_ref[slot, cell], columns[cell])
+        for place, offsets in reached_cells(cells):
+            add_transposed(sums, place, cell, cells, tiles_ref[offsets[0], cell], columns[cell])
     return close_transposed(sums, cells)
 
 
@@ -81,9 +81,9 @@
     found = []
     for cell in range(cells):
         total = None
-        for slot, ((row, shift_z), _) in enumerate(reached_cells(cells)):
+        for (row, shift_z), offsets in reached_cells(cells):
             reached = (cell + shift_z) % cells
-            product = tiles_ref[slot, cell] * rows[row][reached : reached + 1]
+            product = tiles_ref[offsets[0], cell] * rows[row][reached : reached + 1]
             total = product if total is None else total + product
         found.append(jnp.sum(total.T, axis=0, keepdims=True))
     return jnp.concatenate(found, axis=0)
@@ -130,7 +130,7 @@
 def start_kernel(
     grid, tiles_hbm, chi_hbm, species_hbm, counts_hbm, hardness_hbm,
     send_ref, own_ref, residual_ref, diagonal_ref, occupied_ref, tiles_ref,
-    chi_ref, species_ref, counts_ref, hardness_ref, more_ref, small_sem, kept_sem, more_sem,
+    chi_ref, species_ref, counts_ref, hardness_ref, small_sem, tiles_sem,
 ):
     cells, slots = chi_ref.shape
     places = reached_cells(cells)
@@ -147,17 +147,13 @@
     ]
     for copy in small:
         copy.start()
-    copies, spare = [], 0
-    for slot, (_, offsets) in enumerate(places):
-        group = [pltpu.make_async_copy(tiles_hbm.at[offsets[0]], tiles_ref.at[slot], kept_sem.at[slot])]
-        for offset in offsets[1:]:
-            group.append(
-                pltpu.make_async_copy(tiles_hbm.at[offset], more_ref.at[spare], more_sem.at[spare])
-            )
-            spare += 1
-        for copy in group:
-            copy.start()
-        copies.append(group)
+    copies = {}
+    for index, (first, last) in enumerate(CHUNKS):
+        span = pl.ds(first, last - first)
+        copies[last - 1] = pltpu.make_async_copy(
+            tiles_hbm.at[span], tiles_ref.at[span], tiles_sem.at[index]
+        )
+        copies[last - 1].start()
 
     for copy in small:
         copy.wait()
@@ -177,18 +173,19 @@
     diagonal_ref[...] = diagonal
     columns = columns_of(residual)
 
-    sums, spare = {}, 0
-    for slot, (place, offsets) in enumerate(places):
-        for copy in copies[slot]:
-            copy.wait()
-        for cell in range(cells):
-            tile = tiles_ref[slot, cell]
-            for extra in range(len(offsets) - 1):
-                tile = tile + more_ref[spare + extra, cell]
-            if len(offsets) > 1:
-                tiles_ref[slot, cell] = tile
-            add_transposed(sums, place, cell, cells, tile, columns[cell])
-        spare += len(offsets) - 1
+    sums = {}
+    pending = sorted(places, key=lambda item: max(item[1]))
+    for last in sorted(copies):
+        copies[last].wait()
+        while pending and max(pending[0][1]) <= last:
+            place, offsets = pending.pop(0)
+            for cell in range(cells):
+                tile = tiles_ref[offsets[0], cell]
+                for extra in offsets[1:]:
+                    tile = tile + tiles_ref[extra, cell]
+                if len(offsets) > 1:
+                    tiles_ref[offsets[0], cell] = tile
+                add_transposed(sums, place, cell, cells, tile, columns[cell])
     sent = close_transposed(sums, cells)
     put_rows(grid, send_ref, sent, residual)
     own_ref[...] = sent[0, 0]
@@ -238,17 +235,15 @@
         "vAv": (v, diagonal * v + 2.0 * sent[0, 0]), "vAr": (v, ar), "vAw": (v, aw),
         "rAr": (r, ar), "rAw": (r, aw), "wAw": (w, aw),
     }
-    width = slots // FOLD
-    lane = lax.broadcasted_iota(jnp.int32, (FOLD, slots), 1) // width
-    line = lax.broadcasted_iota(jnp.int32, (FOLD, slots), 0)
-    parts = [lanes_of(*pairs[name]) for name in SUMS]
-    parts += [jnp.zeros((1, slots), jnp.float32)] * (FOLD - len(SUMS))
-    block = jnp.concatenate(parts, axis=0)
-    shift = slots // 2
-    while shift >= width:
-        block = block + pltpu.roll(block, shift, 1)
-        shift //= 2
-    packed = jnp.sum(jnp.where(lane == line, block, 0.0), axis=0, keepdims=True)
+    packed = jnp.zeros((1, slots), jnp.float32)
+    for names in (tuple(name for name in SUMS if name != "vAv"), ("vAv",)):
+        block = jnp.concatenate([pairs[name][0] * pairs[name][1] for name in names], axis=0)
+        line = lax.broadcasted_iota(jnp.int32, block.shape, 0) // cells
+        place = jnp.zeros(block.shape, jnp.int32)
+        for index, name in enumerate(names):
+            place = jnp.where(line == index, SUMS.index(name), place)
+        at = lax.broadcasted_iota(jnp.int32, block.shape, 1) == place
+        packed = packed + jnp.sum(jnp.where(at, whole(block), 0.0), axis=0, keepdims=True)
     half = cells // 2
     message = [sent[row] for row in AHEAD] + [v]
     for device in range(send_ref.shape[0]):
@@ -284,34 +279,27 @@
 
 
 def image_kernel(
-    grid, tiles_ref, received_ref, state_ref, own_ref, diagonal_ref, occupied_ref, image_ref
+    grid, tiles_ref, received_ref, residual_ref, first_image_ref, state_ref, own_ref, diagonal_ref,
+    occupied_ref, parts_ref, sums_ref, next_state_ref, next_sums_ref,
 ):
-    v = state_ref[3]
+    r0, w = residual_ref[...], first_image_ref[...]
+    slots = r0.shape[1]
+    aw, r, ar, v = (state_ref[index] for index in range(4))
     ahead, behind = neighbours(grid)
     at_value = len(AHEAD)
     rows = {(0, 0): v}
-    image = diagonal_ref[...] * v + own_ref[...]
+    av = diagonal_ref[...] * v + own_ref[...]
     for place, row in enumerate(AHEAD):
         front, back = ahead[place], behind[place]
         rows[row] = both_halves(received_ref[front, at_value], received_ref[front, at_value + 1])
-        image = image + both_halves(received_ref[back, place], received_ref[back, at_value + 1])
-    image_ref[...] = occupied_ref[...] * (image + direct_products(tiles_ref, rows))
-
-
-def last_kernel(
-    residual_ref, first_image_ref, state_ref, image_ref, parts_ref, crossed_ref, mate_ref, sums_ref,
-    out_charges_ref, out_residual_ref,
-):
-    r0, w, av = residual_ref[...], first_image_ref[...], image_ref[...]
-    slots = r0.shape[1]
-    aw, r, ar, v = (state_ref[index] for index in range(4))
+        av = av + both_halves(received_ref[back, place], received_ref[back, at_value + 1])
+    av = occupied_ref[...] * (av + direct_products(tiles_ref, rows))
+
     parts = parts_ref[...]
-    lane = lax.broadcasted_iota(jnp.int32, (1, slots), 1) // (slots // FOLD)
+    lane = lax.broadcasted_iota(jnp.int32, (1, slots), 1)
     total = {
         name: whole(jnp.where(lane == index, parts, 0.0)) for index, name in enumerate(SUMS)
     }
-    total["vAv"] = total["vAv"] + 2.0 * whole(crossed_ref[...] + mate_ref[...])
-
     norm0, curvature0 = sums_ref[0:1, 0:1], sums_ref[1:2, 0:1]
     step0 = norm0 / curvature0
     norm1 = total["rr"]
@@ -331,16 +319,24 @@
     norm2 = form("vv", "vr", "vw", "rr", "rw", "ww")
     product2 = form("vAv", "vAr", "vAw", "rAr", "rAw", "wAw")
     ratio2 = norm2 / norm1
-    curvature2 = product2 - ratio2 * ratio2 * curvature1
-    step2 = norm2 / curvature2
     residual2 = one * v + two * r + three * w
     image2 = one * av + two * ar + three * aw
     direction1 = r + ratio1 * r0
     push1 = ar + ratio1 * w
-    direction2 = residual2 + ratio2 * direction1
-    push2 = image2 + ratio2 * push1
-    out_charges_ref[...] = step0 * r0 + step1 * direction1 + step2 * direction2
-    out_residual_ref[...] = residual2 - step2 * push2
+    next_state_ref[0] = step0 * r0 + step1 * direction1
+    next_state_ref[1] = residual2
+    next_state_ref[2] = residual2 + ratio2 * direction1
+    next_state_ref[3] = image2 + ratio2 * push1
+    known = product2 - ratio2 * ratio2 * curvature1
+    for index, scalar in enumerate((norm2, known, 2.0 * one * one)):
+        next_sums_ref[index : index + 1] = jnp.broadcast_to(scalar, (1, slots))
+
+
+def last_kernel(state_ref, sums_ref, crossed_ref, mate_ref, out_charges_ref, out_residual_ref):
+    norm, known, weight = (sums_ref[index : index + 1, 0:1] for index in range(3))
+    step = norm / (known + weight * whole(crossed_ref[...] + mate_ref[...]))
+    out_charges_ref[...] = state_ref[0] + step * state_ref[2]
+    out_residual_ref[...] = state_ref[1] - step * state_ref[3]
 
 
 def body(tiles, chi, species, counts, hardness):
@@ -350,7 +346,6 @@
     offsets = own_tiles.shape[0]
     cells, slots = chi.shape[2:]
     assert cells % 2 == 0 and grid[1] % 2 == 0
-    places = len(reached_cells(cells))
     vmem = pl.BlockSpec(memory_space=pltpu.VMEM)
     hbm = pl.BlockSpec(memory_space=pltpu.HBM)
 
@@ -376,17 +371,15 @@
     arguments = [pltpu.with_memory_space_constraint(each, pltpu.HBM) for each in arguments]
     send, own, r0, diagonal, occupied, kept = call(
         functools.partial(start_kernel, grid),
-        (shape(count, cells, slots), value, value, value, value, shape(places, cells, slots, slots)),
+        (shape(count, cells, slots), value, value, value, value, shape(offsets, cells, slots, slots)),
         [hbm] * 5,
         (
             pltpu.VMEM((cells, slots), jnp.float32),
             pltpu.VMEM((cells, slots), jnp.int32),
             pltpu.SMEM((cells,), jnp.int32),
             pltpu.SMEM(hardness.shape, jnp.float32),
-            pltpu.VMEM((max(offsets - places, 1), cells, slots, slots), jnp.float32),
             pltpu.SemaphoreType.DMA((4,)),
-            pltpu.SemaphoreType.DMA((places,)),
-            pltpu.SemaphoreType.DMA((max(offsets - places, 1),)),
+            pltpu.SemaphoreType.DMA((len(CHUNKS),)),
         ),
     )(*arguments)
     received = exchange(send)
@@ -406,12 +399,10 @@
         functools.partial(cross_kernel, grid), (shape(1, slots), shape(1, slots)), [vmem]
     )(received)
     mate = lax.ppermute(crossed, "gy", [(place, place ^ 1) for place in range(grid[1])])
-    (image,) = call(functools.partial(image_kernel, grid), (value,), [vmem] * 6)(
-        kept, received, state, own, diagonal, occupied
-    )
-    charges, residual = call(last_kernel, (value, value), [vmem] * 8)(
-        r0, w, state, image, parts, crossed, mate, sums
-    )
+    state, sums = call(
+        functools.partial(image_kernel, grid), (shape(4, cells, slots), shape(3, slots)), [vmem] * 10
+    )(kept, received, r0, w, state, own, diagonal, occupied, parts, sums)
+    charges, residual = call(last_kernel, (value, value), [vmem] * 4)(state, sums, crossed, mate)
     return charges[None, None], residual[None, None]
 
 

time: 40.4 us -> 39.8 us (0.985)
  Pallas kernels: 4.69 us -> 4.14 us
where the time goes in v5:
time: 39.8 us; the launch traced here: 39.6 us
  blocking collectives  33.8 us (85%)
  Pallas kernels  4.14 us (10%)
  between operations  0.66 us (2%)
  waiting for transfers between devices  0.59 us (1%)
    all_to_all x3, blocking collectives, exchange(): return lax.all_to_all(buffer, ('gx', 'gy'), 0, 0, tiled=True)  33.8 us
    pallas_call x1, Pallas kernels, body(): call(functools.partial(start_kernel, grid), (shape(count, cells, slots),...  1.94 us
  transfers between devices with their start and end apart: 1, of which 1 were waited for; matrix products, arithmetic and copies ran while one was open for 0% of the time, Pallas kernels for 1%

profile of v5, /device:TPU:0, one launch (start us, length us, event | category | flops | bytes accessed | tf_op | source)
XLA Modules:
  0.0 39.6 jit_solution(15215356802908866484)
XLA Ops:
  0.6 1.9 %shard_map.68 = (f32[32,2,128]{2,1,0:T(2,128)S(1)}, f32[2,128]{1,0:T(2,128)S(1)}, f32[2,128]{1,0:T(2,128)S(1)}, f32[2,128]{1,0:T(2,128)S(1)}, f32[2,128]{1,0:T(2,128)S(1)}, /*index=5*/f32[23,2,128,128]{3,2,1,0:T(8,128)S(1)}) custom-call(f32[23,2,128,128]{3,2,1,0:T(8,128)} %bitcast.6, f32[2,128]{1,0:T(2,128)} %bitcast.7, s32[2,128]{1,0:T(2,128)} %bitcast.8, ...), custom_call_target="tpu_custom_call" | custom-call | tf_op jit(solution)/shard_map/pallas_call | solution.py:372
  2.6 14.4 %all_to_all.15.received_ref = f32[32,2,128]{2,1,0:T(2,128)S(1)} all-to-all(f32[32,2,128]{2,1,0:T(2,128)S(1)} %get-tuple-element.22), channel_id=1, replica_groups=mesh['gx'=8,'gy'=4] {'gx','gy'}, dimensions={0} | all-to-all | bytes 65536 | tf_op jit(solution)/shard_map/all_to_all | solution.py:368
  17.0 0.5 %shard_map.69 = (f32[32,4,128]{2,1,0:T(4,128)S(1)}, f32[2,128]{1,0:T(2,128)S(1)}, f32[2,128]{1,0:T(2,128)S(1)}) custom-call(f32[23,2,128,128]{3,2,1,0:T(8,128)S(1)} %get-tuple-element.21.tiles_ref, f32[32,2,128]{2,1,0:T(2,128)S(1)} %all_to_all.15.received_ref, f32[2,128]{1,0:T(2,128)S(1)} %get-tuple-element.23.residual_ref, ...), custom_call_target="tpu_custom_call" | custom-call | tf_op jit(solution)/shard_map/pallas_call | solution.py:386
  17.5 9.1 %all_to_all.16.received_ref = f32[32,4,128]{2,1,0:T(4,128)S(1)} all-to-all(f32[32,4,128]{2,1,0:T(4,128)S(1)} %get-tuple-element.27), channel_id=1, replica_groups=mesh['gx'=8,'gy'=4] {'gx','gy'}, dimensions={0} | all-to-all | bytes 131072 | tf_op jit(solution)/shard_map/all_to_all | solution.py:368
  26.6 0.6 %shard_map.70 = (f32[32,10,1,128]{3,2,1,0:T(1,128)S(1)}, f32[2,128]{1,0:T(2,128)S(1)}, f32[4,2,128]{2,1,0:T(2,128)S(1)}, f32[2,128]{1,0:T(2,128)S(1)}) custom-call(f32[23,2,128,128]{3,2,1,0:T(8,128)S(1)} %get-tuple-element.21.tiles_ref, f32[32,4,128]{2,1,0:T(4,128)S(1)} %all_to_all.16.received_ref, f32[2,128]{1,0:T(2,128)S(1)} %get-tuple-element.23.residual_ref, ...), custom_call_target="tpu_custom_call" | custom-call | tf_op jit(solution)/shard_map/pallas_call | solution.py:392
  27.2 10.3 %all_to_all.17.received_ref = f32[32,10,1,128]{3,2,1,0:T(1,128)S(1)} all-to-all(f32[32,10,1,128]{3,2,1,0:T(1,128)S(1)} %get-tuple-element.30), channel_id=1, replica_groups=mesh['gx'=8,'gy'=4] {'gx','gy'}, dimensions={0} | all-to-all | bytes 327680 | tf_op jit(solution)/shard_map/all_to_all | solution.py:368
  37.5 0.1 shard_map.71
  37.7 0.4 collective-permute-start
  38.0 0.3 shard_map.72
  38.3 0.6 %collective-permute-done.mate_ref = f32[1,128]{1,0:T(1,128)S(1)} collective-permute-done((f32[1,128]{1,0:T(1,128)S(1)}, f32[1,128]{1,0:T(1,128)S(1)}, u32[]{:S(2)}, u32[]{:S(2)}) %collective-permute-start) | collective-permute-done | bytes 544 | tf_op jit(solution)/shard_map/ppermute | solution.py:401
  38.9 0.7 %shard_map.73 = (f32[2,128]{1,0:T(2,128)}, f32[2,128]{1,0:T(2,128)}) custom-call(f32[4,2,128]{2,1,0:T(2,128)S(1)} %get-tuple-element.35.state_ref, f32[3,128]{1,0:T(4,128)S(1)} %get-tuple-element.36.sums_ref, f32[1,128]{1,0:T(1,128)S(1)} %get-tuple-element.37.crossed_ref, f32[1,128]{1,0:T(1,128)S(1)} %collective-permute-done.mate_ref), custom_call_target="tpu_custom_call" | custom-call | tf_op jit(solution)/shard_map/pallas_call | solution.py:405
Async XLA Ops:
  37.7 1.2 %collective-permute-start = (f32[1,128]{1,0:T(1,128)S(1)}, f32[1,128]{1,0:T(1,128)S(1)}, u32[]{:S(2)}, u32[]{:S(2)}) collective-permute-start(f32[1,128]{1,0:T(1,128)S(1)} %get-tuple-element.37.crossed_ref), channel_id=1, source_target_pairs={{0,1},{1,0},{2,3},{3,2},{4,5},{5,4},{6,7},{7,6},{8,9},{9,8},{10,11... | collective-permute-start | bytes 1544 | tf_op jit(solution)/shard_map/ppermute | solution.py:401

commit v6 on v5

--- a/solution.py
+++ b/solution.py
@@ -129,7 +129,7 @@
 
 def start_kernel(
     grid, tiles_hbm, chi_hbm, species_hbm, counts_hbm, hardness_hbm,
-    send_ref, own_ref, residual_ref, diagonal_ref, occupied_ref, tiles_ref,
+    send_ref, own_ref, residual_ref, diagonal_ref, occupied_ref, guess_ref, tiles_ref,
     chi_ref, species_ref, counts_ref, hardness_ref, small_sem, tiles_sem,
 ):
     cells, slots = chi_ref.shape
@@ -166,8 +166,12 @@
     residual = -chi_ref[...] * occupied
     species = species_ref[...]
     diagonal = jnp.zeros_like(residual)
+    least, most = hardness_ref[0], hardness_ref[0]
     for element in range(hardness_ref.shape[0]):
         diagonal = diagonal + jnp.where(species == element, hardness_ref[element], 0.0)
+        least = jnp.minimum(least, hardness_ref[element])
+        most = jnp.maximum(most, hardness_ref[element])
+    guess_ref[...] = 2.0 / jnp.full((1, slots), least + most, jnp.float32)
     occupied_ref[...] = occupied
     residual_ref[...] = residual
     diagonal_ref[...] = diagonal
@@ -192,8 +196,8 @@
 
 
 def first_kernel(
-    grid, tiles_ref, received_ref, residual_ref, own_ref, diagonal_ref, occupied_ref,
-    send_ref, next_own_ref, image_ref,
+    grid, tiles_ref, received_ref, residual_ref, own_ref, diagonal_ref, occupied_ref, guess_ref,
+    send_ref, next_own_ref, image_ref, reduced_ref,
 ):
     residual = residual_ref[...]
     cells = residual.shape[0]
@@ -202,27 +206,30 @@
     )
     image_ref[...] = image
     parts = jnp.concatenate([lanes_of(residual, residual), lanes_of(residual, image)], axis=0)
-    sent = transposed_products(tiles_ref, image)
+    reduced = residual - guess_ref[...] * image
+    reduced_ref[...] = reduced
+    sent = transposed_products(tiles_ref, reduced)
     next_own_ref[...] = sent[0, 0]
     count = send_ref.shape[0]
     send_ref[:, cells : cells + 2, :] = jnp.broadcast_to(parts[None], (count,) + parts.shape)
-    put_rows(grid, send_ref, sent, image)
+    put_rows(grid, send_ref, sent, reduced)
 
 
 def second_kernel(
-    grid, tiles_ref, received_ref, residual_ref, image_ref, own_ref, diagonal_ref, occupied_ref,
-    send_ref, next_own_ref, state_ref, sums_ref,
+    grid, tiles_ref, received_ref, residual_ref, image_ref, reduced_ref, own_ref, diagonal_ref,
+    occupied_ref, guess_ref, send_ref, next_own_ref, state_ref, sums_ref,
 ):
-    r0, w = residual_ref[...], image_ref[...]
+    r0, w, u, guess = residual_ref[...], image_ref[...], reduced_ref[...], guess_ref[...]
     cells, slots = r0.shape
     diagonal = diagonal_ref[...]
-    aw = applied(grid, tiles_ref, received_ref, w, own_ref[...], diagonal, occupied_ref[...])
+    au = applied(grid, tiles_ref, received_ref, u, own_ref[...], diagonal, occupied_ref[...])
     totals = whole(jnp.sum(received_ref[:, cells : cells + 2, :], axis=0))
     norm, curvature = totals[0:1], totals[1:2]
-    step = norm / curvature
-    r = r0 - step * w
-    ar = w - step * aw
-    v = r - step * ar
+    share = norm / curvature / guess
+    r = share * u + (1.0 - share) * r0
+    ar = share * au + (1.0 - share) * w
+    aw = (w - au) / guess
+    v = r - guess * ar
     sent = transposed_products(tiles_ref, v)
     next_own_ref[...] = sent[0, 0]
     for index, value in enumerate((aw, r, ar, v)):
@@ -280,7 +287,7 @@
 
 def image_kernel(
     grid, tiles_ref, received_ref, residual_ref, first_image_ref, state_ref, own_ref, diagonal_ref,
-    occupied_ref, parts_ref, sums_ref, next_state_ref, next_sums_ref,
+    occupied_ref, parts_ref, sums_ref, guess_ref, next_state_ref, next_sums_ref,
 ):
     r0, w = residual_ref[...], first_image_ref[...]
     slots = r0.shape[1]
@@ -306,7 +313,7 @@
     ratio1 = norm1 / norm0
     curvature1 = total["rAr"] - ratio1 * ratio1 * curvature0
     step1 = norm1 / curvature1
-    one = step1 / step0
+    one = step1 / guess_ref[:, 0:1]
     two = 1.0 - one
     three = -step1 * ratio1
 
@@ -369,9 +376,9 @@
 
     arguments = (own_tiles, chi[0, 0], species[0, 0], counts[0, 0], hardness)
     arguments = [pltpu.with_memory_space_constraint(each, pltpu.HBM) for each in arguments]
-    send, own, r0, diagonal, occupied, kept = call(
+    send, own, r0, diagonal, occupied, guess, kept = call(
         functools.partial(start_kernel, grid),
-        (shape(count, cells, slots), value, value, value, value, shape(offsets, cells, slots, slots)),
+        (shape(count, cells, slots), value, value, value, value, shape(1, slots), shape(offsets, cells, slots, slots)),
         [hbm] * 5,
         (
             pltpu.VMEM((cells, slots), jnp.float32),
@@ -383,25 +390,25 @@
         ),
     )(*arguments)
     received = exchange(send)
-    send, own, w = call(
+    send, own, w, u = call(
         functools.partial(first_kernel, grid),
-        (shape(count, cells + 2, slots), value, value),
-        [vmem] * 6,
-    )(kept, received, r0, own, diagonal, occupied)
+        (shape(count, cells + 2, slots), value, value, value),
+        [vmem] * 7,
+    )(kept, received, r0, own, diagonal, occupied, guess)
     received = exchange(send)
     send, own, state, sums = call(
         functools.partial(second_kernel, grid),
         (shape(count, len(AHEAD) + 3, cells // 2, slots), value, shape(4, cells, slots), shape(2, slots)),
-        [vmem] * 7,
-    )(kept, received, r0, w, own, diagonal, occupied)
+        [vmem] * 9,
+    )(kept, received, r0, w, u, own, diagonal, occupied, guess)
     received = exchange(send)
     crossed, parts = call(
         functools.partial(cross_kernel, grid), (shape(1, slots), shape(1, slots)), [vmem]
     )(received)
     mate = lax.ppermute(crossed, "gy", [(place, place ^ 1) for place in range(grid[1])])
     state, sums = call(
-        functools.partial(image_kernel, grid), (shape(4, cells, slots), shape(3, slots)), [vmem] * 10
-    )(kept, received, r0, w, state, own, diagonal, occupied, parts, sums)
+        functools.partial(image_kernel, grid), (shape(4, cells, slots), shape(3, slots)), [vmem] * 11
+    )(kept, received, r0, w, state, own, diagonal, occupied, parts, sums, guess)
     charges, residual = call(last_kernel, (value, value), [vmem] * 4)(state, sums, crossed, mate)
     return charges[None, None], residual[None, None]
 

time: 39.8 us -> 39.8 us (level)
  no operation moved by 1% of the time
where the time goes in v6:
time: 39.8 us; the launch traced here: 39.6 us
  blocking collectives  33.8 us (85%)
  Pallas kernels  4.16 us (10%)
  between operations  0.66 us (2%)
  waiting for transfers between devices  0.59 us (1%)
    all_to_all x3, blocking collectives, exchange(): return lax.all_to_all(buffer, ('gx', 'gy'), 0, 0, tiled=True)  33.8 us
    pallas_call x1, Pallas kernels, body(): call(functools.partial(start_kernel, grid), (shape(count, cells, slots),...  1.94 us
  transfers between devices with their start and end apart: 1, of which 1 were waited for; matrix products, arithmetic and copies ran while one was open for 0% of the time, Pallas kernels for 1%

profile of v6, /device:TPU:0, one launch (start us, length us, event | category | flops | bytes accessed | tf_op | source)
XLA Modules:
  0.0 39.6 jit_solution(6794889655160833131)
XLA Ops:
  0.6 1.9 %shard_map.68 = (f32[32,2,128]{2,1,0:T(2,128)S(1)}, f32[2,128]{1,0:T(2,128)S(1)}, f32[2,128]{1,0:T(2,128)S(1)}, f32[2,128]{1,0:T(2,128)S(1)}, f32[2,128]{1,0:T(2...) custom-call(f32[23,2,128,128]{3,2,1,0:T(8,128)} %bitcast.6, f32[2,128]{1,0:T(2,128)} %bitcast.7, ...), custom_call_target="tpu_custom_call" | custom-call | tf_op jit(solution)/shard_map/pallas_call | solution.py:379
  2.6 14.4 %all_to_all.15.received_ref = f32[32,2,128]{2,1,0:T(2,128)S(1)} all-to-all(f32[32,2,128]{2,1,0:T(2,128)S(1)} %get-tuple-element.24), channel_id=1, replica_groups=mesh['gx'=8,'gy'=4] {'gx','gy'}, dimensions={0} | all-to-all | bytes 65536 | tf_op jit(solution)/shard_map/all_to_all | solution.py:375
  17.0 0.5 %shard_map.69 = (f32[32,4,128]{2,1,0:T(4,128)S(1)}, f32[2,128]{1,0:T(2,128)S(1)}, f32[2,128]{1,0:T(2,128)S(1)}, f32[2,128]{1,0:T(2,128)S(1)}) custom-call(f32[23,2,128,128]{3,2,1,0:T(8,128)S(1)} %get-tuple-element.23.tiles_ref, f32[32,2,128]{2,1,0:T(2,128)S(1)} %all_to_all.15.received_ref, f32[2,128]{1,0:T(2,128)S(1)} %get-tuple-element.25.residual_ref, ...), custom_call_target="tpu_custom_call" | custom-call | tf_op jit(solution)/shard_map/pallas_call | solution.py:393
  17.5 9.1 %all_to_all.16.received_ref = f32[32,4,128]{2,1,0:T(4,128)S(1)} all-to-all(f32[32,4,128]{2,1,0:T(4,128)S(1)} %get-tuple-element.30), channel_id=1, replica_groups=mesh['gx'=8,'gy'=4] {'gx','gy'}, dimensions={0} | all-to-all | bytes 131072 | tf_op jit(solution)/shard_map/all_to_all | solution.py:375
  26.6 0.7 %shard_map.70 = (f32[32,10,1,128]{3,2,1,0:T(1,128)S(1)}, f32[2,128]{1,0:T(2,128)S(1)}, f32[4,2,128]{2,1,0:T(2,128)S(1)}, f32[2,128]{1,0:T(2,128)S(1)}) custom-call(f32[23,2,128,128]{3,2,1,0:T(8,128)S(1)} %get-tuple-element.23.tiles_ref, f32[32,4,128]{2,1,0:T(4,128)S(1)} %all_to_all.16.received_ref, f32[2,128]{1,0:T(2,128)S(1)} %get-tuple-element.25.residual_ref, ...), custom_call_target="tpu_custom_call" | custom-call | tf_op jit(solution)/shard_map/pallas_call | solution.py:399
  27.2 10.3 %all_to_all.17.received_ref = f32[32,10,1,128]{3,2,1,0:T(1,128)S(1)} all-to-all(f32[32,10,1,128]{3,2,1,0:T(1,128)S(1)} %get-tuple-element.34), channel_id=1, replica_groups=mesh['gx'=8,'gy'=4] {'gx','gy'}, dimensions={0} | all-to-all | bytes 327680 | tf_op jit(solution)/shard_map/all_to_all | solution.py:375
  37.6 0.1 shard_map.71
  37.7 0.4 collective-permute-start
  38.1 0.3 shard_map.72
  38.3 0.6 %collective-permute-done.mate_ref = f32[1,128]{1,0:T(1,128)S(1)} collective-permute-done((f32[1,128]{1,0:T(1,128)S(1)}, f32[1,128]{1,0:T(1,128)S(1)}, u32[]{:S(2)}, u32[]{:S(2)}) %collective-permute-start) | collective-permute-done | bytes 544 | tf_op jit(solution)/shard_map/ppermute | solution.py:408
  38.9 0.7 %shard_map.73 = (f32[2,128]{1,0:T(2,128)}, f32[2,128]{1,0:T(2,128)}) custom-call(f32[4,2,128]{2,1,0:T(2,128)S(1)} %get-tuple-element.39.state_ref, f32[3,128]{1,0:T(4,128)S(1)} %get-tuple-element.40.sums_ref, f32[1,128]{1,0:T(1,128)S(1)} %get-tuple-element.41.crossed_ref, f32[1,128]{1,0:T(1,128)S(1)} %collective-permute-done.mate_ref), custom_call_target="tpu_custom_call" | custom-call | tf_op jit(solution)/shard_map/pallas_call | solution.py:412
Async XLA Ops:
  37.7 1.2 %collective-permute-start = (f32[1,128]{1,0:T(1,128)S(1)}, f32[1,128]{1,0:T(1,128)S(1)}, u32[]{:S(2)}, u32[]{:S(2)}) collective-permute-start(f32[1,128]{1,0:T(1,128)S(1)} %get-tuple-element.41.crossed_ref), channel_id=1, source_target_pairs={{0,1},{1,0},{2,3},{3,2},{4,5},{5,4},{6,7},{7,6},{8,9},{9,8},{10,11... | collective-permute-start | bytes 1544 | tf_op jit(solution)/shard_map/ppermute | solution.py:408
